TPU v7x, 256 devices: a whole 4x4x8 slice. The times are simulated.
256 devices in a mesh: visit: 32 (over z_lo, y, core), tile: 8 (over z_hi, x).
Axes of the slice: x: 4, y: 4, z: 8 (z_hi: 2, z_lo: 4; z = z_hi * 4 + z_lo), core: 2. Of those that a mesh axis runs over, the one named last changes fastest.
Arguments:
- exposures: float32 [32, 2048, 256], P('visit', 'tile'), may hold values from 0.3 to 3
- sky_model: float32 [2048, 256], P(('tile', 'visit')), may hold values from 0.5 to 2
- blur_kernels: float32 [32, 31, 31], P('visit'), may hold values from 0.05 to 1
- coverage: int32 [32, 8], P('visit'), may hold values from 0 to 1, as said below
Outputs:
- deconvolved: float32 [2048, 256], P(('tile', 'visit'))
Inputs may be any that keep to these rules, and one draw needn't show every extreme that they name: `coverage`: every tile is covered by at least one exposure.
All inputs are finite; a program needn't handle non-finite values.
Results may differ from a plain program's by a relative error of at most 0.0001.
Values sent between devices are 32-bit elements; how exact they have to be, the bound alone decides.
A program may use at most 128 MiB of HBM per device.

v0:
```python
import jax
import jax.numpy as jnp
from jax import lax
from jax.sharding import PartitionSpec as P

ITERS = 2


def padded(array, sides, width):
    for axis, dim in sides:
        peers, length = (lax.axis_size(axis), array.shape[dim])
        up = [(i, (i + 1) % peers) for i in range(peers - 1)]
        down = [(j, i) for i, j in up]
        last = lax.slice_in_dim(array, length - width, length, axis=dim)
        initial = lax.slice_in_dim(array, 0, width, axis=dim)
        before = lax.ppermute(last, axis, up)
        after = lax.ppermute(initial, axis, down)
        array = jnp.concatenate([before, array, after], axis=dim)
    return array


def band_lookup(width, kernel_len):
    half = kernel_len // 2
    differ = jnp.arange(width)[:, None] - jnp.arange(width)[None, :] + half
    band_table = (differ[:, :, None] == jnp.arange(kernel_len)[None, None, :]).astype(jnp.float32)
    return band_table.reshape(width * width, kernel_len)


def column_operator(kernel, band_table, width):
    kernel_len = kernel.shape[0]
    operator = jnp.dot(band_table, kernel.T, precision=lax.Precision.HIGHEST)
    operator = operator.reshape(width, width, kernel_len).transpose(0, 2, 1)
    return operator.reshape(width, kernel_len * width)


def correlate(extended, operator):
    width = operator.shape[0]
    kernel_len = operator.shape[1] // width
    out_rows = extended.shape[0] - (kernel_len - 1)
    product = jnp.dot(extended, operator, precision=lax.Precision.HIGHEST)
    product = product.reshape(extended.shape[0], kernel_len, width)
    total = product[0:out_rows, 0]
    for offset in range(1, kernel_len):
        total = total + product[offset : offset + out_rows, offset]
    return total


def body(exposures, sky_model, blur_kernels, coverage):
    tile_rows = exposures.shape[1]
    tile_cols = exposures.shape[2]
    kernel_len = blur_kernels.shape[1]
    radius = kernel_len // 2
    tile_count = lax.axis_size("tile")
    tile_place = lax.axis_index("tile")
    kernels = blur_kernels / jnp.sum(blur_kernels, axis=(1, 2), keepdims=True)
    band_table = band_lookup(tile_cols, kernel_len)
    forward_ops = [column_operator(kernels[0], band_table, tile_cols)]
    flipped_ops = [column_operator(kernels[0][::-1, ::-1], band_table, tile_cols)]
    global_row = tile_place * tile_rows - radius + jnp.arange(tile_rows + 2 * radius)
    row_owner = jnp.floor_divide(global_row, tile_rows)
    selector = (row_owner[:, None] == jnp.arange(tile_count)[None, :]).astype(jnp.float32)
    weight_rows = jnp.dot(coverage.astype(jnp.float32), selector.T, precision=lax.Precision.HIGHEST)
    own_weights = weight_rows[:, radius : radius + tile_rows]
    member = 0
    column_sums = forward_ops[member].reshape(tile_cols, kernel_len, tile_cols).sum(axis=0)
    row_window = jnp.stack(
        [weight_rows[member][offset : offset + tile_rows] for offset in range(kernel_len)], axis=1
    )
    norm_local = jnp.dot(row_window, column_sums, precision=lax.Precision.HIGHEST)
    norm_shard = lax.psum_scatter(norm_local, "visit", scatter_dimension=0, tiled=True)
    model_shard = sky_model
    for step in range(ITERS):
        whole = lax.all_gather(model_shard, "visit", axis=0, tiled=True)
        model_wide = padded(whole, (("tile", 0),), radius)
        member = 0
        blurred = correlate(model_wide, flipped_ops[member])
        ratio_list = [own_weights[member][:, None] * exposures[member] / blurred]
        ratios = jnp.stack(ratio_list)
        ratio_wide = padded(ratios, (("tile", 1),), radius)
        member = 0
        numerator = correlate(ratio_wide[member], forward_ops[member])
        update = lax.psum_scatter(numerator, "visit", scatter_dimension=0, tiled=True)
        model_shard = model_shard * update / norm_shard
    return model_shard


def solution(mesh):
    return jax.shard_map(
        body,
        mesh=mesh,
        in_specs=(
            P("visit", "tile", None),
            P(("tile", "visit"), None),
            P("visit", None, None),
            P("visit", None),
        ),
        out_specs=P(("tile", "visit"), None),
        check_vma=False,
    )
```

profile of v0, /device:TPU:6, one launch (start us, length us, event | category | flops | bytes accessed | tf_op | source)
XLA Modules:
  0.0 642.9 jit_solution(17559654957804409515)
XLA Ops:
  6.5 0.0 reduce-scatter.6.cloned.1.call-start
  6.5 45.5 %all_gather.6 = f32[256,256]{1,0:T(8,128)S(1)} all-gather(f32[8,256]{1,0:T(8,128)} %param.5), channel_id=1, replica_groups=mesh['visit'=32,'tile'=8] {'visit'}, dimensions={0}, use_global_device_ids=true | all-gather | bytes 270336 | tf_op jit(solution)/shard_map/all_gather | solution.py:73
  52.1 6.3 collective-permute-start
  58.4 1.9 collective-permute-start.1
  60.4 1.4 reduce_sum.18
  61.7 1.4 broadcast_divide_fusion
  63.1 0.1 rev.3
  63.2 0.9 fusion.116
  64.2 0.1 fusion.114
  64.2 6.3 fusion.117
  70.6 6.1 fusion.17
  76.6 0.1 fusion.115
  76.7 0.1 slice.660
  76.8 10.0 %copy.7 = f32[256,31,256]{0,2,1:T(8,128)} copy(f32[256,31,256]{2,1,0:T(8,128)} %fusion.17) | data formatting | bytes 16252928 | tf_op jit(solution)/shard_map/transpose | solution.py:32
  86.7 0.1 stack.129
  86.8 0.0 copy-start
  86.9 0.0 collective-permute-done
  86.9 0.0 collective-permute-done.1
  86.9 11.2 %fusion.10 = f32[286,31,256]{2,0,1:T(8,128)S(1)} fusion(f32[256,31,256]{0,2,1:T(8,128)} %copy.7, f32[15,256]{1,0:T(8,128)S(1)} %collective-permute-done.1, f32[256,256]{1,0:T(8,128)S(1)} %all_gather.6, f32[15,256]{1,0:T(8,128)S(1)} %collective-permute-done), kind=kOutput, calls=%fused_computation.11 | convolution fusion | flops 6972652544 | bytes 17498112 | tf_op jit(solution)/shard_map/dot_general | solution.py:40
  98.1 0.0 copy-done
  98.1 0.8 fusion.81
  98.9 9.9 %collective-permute-start.2 = (f32[1,15,256]{2,1,0:T(8,128)S(1)}, f32[1,15,256]{2,1,0:T(8,128)S(1)}, u32[]{:S(2)}, u32[]{:S(2)}) collective-permute-start(f32[1,15,256]{2,1,0:T(8,128)S(1)} %get-tuple-element.9), channel_id=1, source_target_pairs={{0,1},{1,2},{2,3},{3,4},{4,5},{5,6},{6,7},{8,9},{9,10},{10,11},{11... | collective-permute-start | bytes 46088 | tf_op jit(solution)/shard_map/ppermute | solution.py:16
  108.9 1.9 collective-permute-start.3
  110.8 1.1 fusion.118
  111.9 0.0 reduce-scatter.6.cloned.1.call-update
  112.0 0.2 reduce-scatter.4.cloned.1.call-start
  112.2 9.9 %copy.8 = f32[256,31,256]{0,2,1:T(8,128)} copy(f32[256,31,256]{2,1,0:T(8,128)} %get-tuple-element.47) | data formatting | bytes 16252928 | tf_op jit(solution)/shard_map/transpose | solution.py:32
  122.1 0.0 collective-permute-done.2
  122.1 0.0 collective-permute-done.3
  122.1 11.2 %fusion.6 = f32[286,31,256]{2,0,1:T(8,128)S(1)} fusion(f32[256,31,256]{0,2,1:T(8,128)} %copy.8, f32[1,15,256]{2,1,0:T(8,128)S(1)} %collective-permute-done.3, f32[1,256,256]{2,1,0:T(8,128)S(1)} %fusion.81, f32[1,15,256]{2,1,0:T(8,128)S(1)} %collective-permute-done.2), kind=kOutput, calls=%fused_computation.7 | convolution fusion | flops 6972652544 | bytes 17498112 | tf_op jit(solution)/shard_map/dot_general | solution.py:40
  133.3 0.0 copy-start.1
  133.3 1.4 fusion.65
  134.7 0.0 reduce-scatter.4.cloned.1.call-update
  134.8 0.0 reduce-scatter.8.cloned.1.call-start
  134.8 121.9 %reduce-scatter.6.cloned.1.call-done = f32[8,256]{1,0:T(8,128)} async-done(((f32[256,256]{1,0:T(8,128)}), f32[8,256]{1,0:T(8,128)}) %reduce-scatter.6.cloned.1.call-update) | async-done | bytes 8208 | tf_op jit(solution)/shard_map/reduce_scatter | solution.py:70
  256.7 144.6 %reduce-scatter.4.cloned.1.call-done = f32[8,256]{1,0:T(8,128)} async-done(((f32[256,256]{1,0:T(8,128)}), f32[8,256]{1,0:T(8,128)}) %reduce-scatter.4.cloned.1.call-update) | async-done | bytes 8208 | tf_op jit(solution)/shard_map/reduce_scatter | solution.py:82
  401.3 0.0 copy-done.1
  401.3 0.7 multiply_divide_fusion.1
  402.0 38.3 %all_gather.7 = f32[256,256]{1,0:T(8,128)S(1)} all-gather(f32[8,256]{1,0:T(8,128)S(1)} %multiply_divide_fusion.1), channel_id=1, replica_groups=mesh['visit'=32,'tile'=8] {'visit'}, dimensions={0}, use_global_device_ids=true | all-gather | bytes 270336 | tf_op jit(solution)/shard_map/all_gather | solution.py:73
  440.3 4.5 collective-permute-start.4
  444.8 1.9 collective-permute-start.5
  446.7 0.0 collective-permute-done.4
  446.7 9.7 %collective-permute-done.5 = f32[15,256]{1,0:T(8,128)S(1)} collective-permute-done((f32[15,256]{1,0:T(8,128)S(1)}, f32[15,256]{1,0:T(8,128)S(1)}, u32[]{:S(2)}, u32[]{:S(2)}) %collective-permute-start.5) | collective-permute-done | bytes 15392 | tf_op jit(solution)/shard_map/ppermute | solution.py:17
  456.4 11.2 %fusion.8 = f32[286,31,256]{2,0,1:T(8,128)S(1)} fusion(f32[256,31,256]{0,2,1:T(8,128)} %copy.7, f32[15,256]{1,0:T(8,128)S(1)} %collective-permute-done.5, f32[256,256]{1,0:T(8,128)S(1)} %all_gather.7, f32[15,256]{1,0:T(8,128)S(1)} %collective-permute-done.4), kind=kOutput, calls=%fused_computation.9 | convolution fusion | flops 6972652544 | bytes 17498112 | tf_op jit(solution)/shard_map/dot_general | solution.py:40
  467.6 0.8 fusion.50
  468.4 1.9 collective-permute-start.6
  470.4 4.1 collective-permute-start.7
  474.5 0.0 collective-permute-done.6
  474.5 7.5 %collective-permute-done.7 = f32[1,15,256]{2,1,0:T(8,128)S(1)} collective-permute-done((f32[1,15,256]{2,1,0:T(8,128)S(1)}, f32[1,15,256]{2,1,0:T(8,128)S(1)}, u32[]{:S(2)}, u32[]{:S(2)}) %collective-permute-start.7) | collective-permute-done | bytes 15392 | tf_op jit(solution)/shard_map/ppermute | solution.py:17
  482.0 11.2 %fusion.4 = f32[286,31,256]{2,0,1:T(8,128)S(1)} fusion(f32[256,31,256]{0,2,1:T(8,128)} %copy.8, f32[1,15,256]{2,1,0:T(8,128)S(1)} %collective-permute-done.7, f32[1,256,256]{2,1,0:T(8,128)S(1)} %fusion.50, f32[1,15,256]{2,1,0:T(8,128)S(1)} %collective-permute-done.6), kind=kOutput, calls=%fused_computation.5 | convolution fusion | flops 6972652544 | bytes 17498112 | tf_op jit(solution)/shard_map/dot_general | solution.py:40
  493.2 0.0 copy-start.2
  493.2 1.4 fusion.34
  494.6 0.0 reduce-scatter.8.cloned.1.call-update
  494.7 140.4 %reduce-scatter.8.cloned.1.call-done = f32[8,256]{1,0:T(8,128)} async-done(((f32[256,256]{1,0:T(8,128)}), f32[8,256]{1,0:T(8,128)}) %reduce-scatter.8.cloned.1.call-update) | async-done | bytes 8208 | tf_op jit(solution)/shard_map/reduce_scatter | solution.py:82
  635.1 0.0 copy-done.2
  635.1 1.3 multiply_divide_fusion
  (7 shorter events, 0.1 us)
Async XLA Ops:
  6.5 250.2 %reduce-scatter.6.cloned.1.call-start = ((), (), s32[]{:S(2)}) async-start(), calls=%async_computation.4 | async-start | bytes 270336 | tf_op jit(solution)/shard_map/reduce_scatter | solution.py:70
  52.1 34.8 %collective-permute-start = (f32[15,256]{1,0:T(8,128)S(1)}, f32[15,256]{1,0:T(8,128)S(1)}, u32[]{:S(2)}, u32[]{:S(2)}) collective-permute-start(f32[15,256]{1,0:T(8,128)S(1)} %get-tuple-element.11), channel_id=1, source_target_pairs={{0,1},{1,2},{2,3},{3,4},{4,5},{5,6},{6,7},{8,9},{9,10},{10,11},{11... | collective-permute-start | bytes 46088 | tf_op jit(solution)/shard_map/ppermute | solution.py:16
  58.4 28.5 %collective-permute-start.1 = (f32[15,256]{1,0:T(8,128)S(1)}, f32[15,256]{1,0:T(8,128)S(1)}, u32[]{:S(2)}, u32[]{:S(2)}) collective-permute-start(f32[15,256]{1,0:T(8,128)S(1)} %get-tuple-element.12), channel_id=1, source_target_pairs={{1,0},{2,1},{3,2},{4,3},{5,4},{6,5},{7,6},{9,8},{10,9},{11,10},{12... | collective-permute-start | bytes 46088 | tf_op jit(solution)/shard_map/ppermute | solution.py:17
  86.8 11.3 %copy-start = (f32[1,256,256]{2,1,0:T(8,128)S(1)}, f32[1,256,256]{2,1,0:T(8,128)}, u32[]{:S(2)}) copy-start(f32[1,256,256]{2,1,0:T(8,128)} %param.4) | copy-start | bytes 786436
  98.9 23.2 %collective-permute-start.2 = (f32[1,15,256]{2,1,0:T(8,128)S(1)}, f32[1,15,256]{2,1,0:T(8,128)S(1)}, u32[]{:S(2)}, u32[]{:S(2)}) collective-permute-start(f32[1,15,256]{2,1,0:T(8,128)S(1)} %get-tuple-element.9), channel_id=1, source_target_pairs={{0,1},{1,2},{2,3},{3,4},{4,5},{5,6},{6,7},{8,9},{9,10},{10,11},{11... | collective-permute-start | bytes 46088 | tf_op jit(solution)/shard_map/ppermute | solution.py:16
  108.9 13.2 %collective-permute-start.3 = (f32[1,15,256]{2,1,0:T(8,128)S(1)}, f32[1,15,256]{2,1,0:T(8,128)S(1)}, u32[]{:S(2)}, u32[]{:S(2)}) collective-permute-start(f32[1,15,256]{2,1,0:T(8,128)S(1)} %get-tuple-element.10), channel_id=1, source_target_pairs={{1,0},{2,1},{3,2},{4,3},{5,4},{6,5},{7,6},{9,8},{10,9},{11,10},{12... | collective-permute-start | bytes 46088 | tf_op jit(solution)/shard_map/ppermute | solution.py:17
  112.0 289.3 %reduce-scatter.4.cloned.1.call-start = ((), (), s32[]{:S(2)}) async-start(), calls=%async_computation.3 | async-start | bytes 270336 | tf_op jit(solution)/shard_map/reduce_scatter | solution.py:82
  133.3 268.0 %copy-start.1 = (f32[8,256]{1,0:T(8,128)S(1)}, f32[8,256]{1,0:T(8,128)}, u32[]{:S(2)}) copy-start(f32[8,256]{1,0:T(8,128)} %param.5) | copy-start | bytes 24580
  134.8 500.3 %reduce-scatter.8.cloned.1.call-start = ((), (), s32[]{:S(2)}) async-start(), calls=%async_computation.5 | async-start | bytes 270336 | tf_op jit(solution)/shard_map/reduce_scatter | solution.py:82
  440.3 6.4 %collective-permute-start.4 = (f32[15,256]{1,0:T(8,128)S(1)}, f32[15,256]{1,0:T(8,128)S(1)}, u32[]{:S(2)}, u32[]{:S(2)}) collective-permute-start(f32[15,256]{1,0:T(8,128)S(1)} %get-tuple-element.7), channel_id=1, source_target_pairs={{0,1},{1,2},{2,3},{3,4},{4,5},{5,6},{6,7},{8,9},{9,10},{10,11},{11... | collective-permute-start | bytes 46088 | tf_op jit(solution)/shard_map/ppermute | solution.py:16
  444.8 11.6 %collective-permute-start.5 = (f32[15,256]{1,0:T(8,128)S(1)}, f32[15,256]{1,0:T(8,128)S(1)}, u32[]{:S(2)}, u32[]{:S(2)}) collective-permute-start(f32[15,256]{1,0:T(8,128)S(1)} %get-tuple-element.8), channel_id=1, source_target_pairs={{1,0},{2,1},{3,2},{4,3},{5,4},{6,5},{7,6},{9,8},{10,9},{11,10},{12... | collective-permute-start | bytes 46088 | tf_op jit(solution)/shard_map/ppermute | solution.py:17
  468.4 6.1 collective-permute-start.6
  470.4 11.6 %collective-permute-start.7 = (f32[1,15,256]{2,1,0:T(8,128)S(1)}, f32[1,15,256]{2,1,0:T(8,128)S(1)}, u32[]{:S(2)}, u32[]{:S(2)}) collective-permute-start(f32[1,15,256]{2,1,0:T(8,128)S(1)} %get-tuple-element.6), channel_id=1, source_target_pairs={{1,0},{2,1},{3,2},{4,3},{5,4},{6,5},{7,6},{9,8},{10,9},{11,10},{12... | collective-permute-start | bytes 46088 | tf_op jit(solution)/shard_map/ppermute | solution.py:17
  493.2 141.9 %copy-start.2 = (f32[8,256]{1,0:T(8,128)S(1)}, f32[8,256]{1,0:T(8,128)}, u32[]{:S(2)}) copy-start(f32[8,256]{1,0:T(8,128)} %reduce-scatter.6.cloned.1.call-done) | copy-start | bytes 24580
Sparse Core Ops, SparseCore 0:
  112.1 144.6 reduce-scatter.5
  259.2 142.0 reduce-scatter.3
  494.8 140.2 reduce-scatter.7
where the time goes:
time: 644 us; the launch traced here: 643 us
  waiting for transfers between devices  424 us (66%)
  blocking collectives  83.8 us (13%)
  matrix products  59.2 us (9%)
  starting transfers between devices  32.8 us (5%)
  local copies, waits for them, and re-layouts  20.3 us (3%)
  between operations  13.3 us (2%)
  other arithmetic  9.28 us (1%)
    reduce_scatter x2, waiting for transfers between devices, body(): lax.psum_scatter(numerator, 'visit', scatter_dimension=0, tiled=True)  285 us
    reduce_scatter x1, waiting for transfers between devices, body(): lax.psum_scatter(norm_local, 'visit', scatter_dimension=0, tiled=True)  122 us
    all_gather x2, blocking collectives, body(): whole = lax.all_gather(model_shard, 'visit', axis=0, tiled=True)  83.8 us
    dot_general x4, matrix products, correlate(): product = jnp.dot(extended, operator, precision=lax.Precision.HIGHEST)  44.8 us
    ppermute x4, starting transfers between devices, padded(): before = lax.ppermute(last, axis, up)  22.7 us
    transpose x2, local copies, waits for them, and re-layouts, column_operator(): operator = operator.reshape(width, width, kernel_len).transpose(0, 2, 1)  19.9 us
    ppermute x4, waiting for transfers between devices, padded(): after = lax.ppermute(initial, axis, down)  17.2 us
  transfers between devices with their start and end apart: 11, of which 5 were waited for; matrix products, arithmetic and copies ran while one was open for 8% of the time, Pallas kernels for 0%

commit v1 on v0

v1 whole, which is shorter than its diff:
```python
import jax
import jax.numpy as jnp
from jax import lax
from jax.experimental import pallas as pl
from jax.experimental.pallas import tpu as pltpu
from jax.sharding import PartitionSpec as P

F32 = jnp.float32
BF = jnp.bfloat16
HI = lax.Precision.HIGHEST
MESH = pl.DeviceIdType.MESH
ITERS = 2


def iota(shape, dim):
    return lax.broadcasted_iota(jnp.int32, shape, dim)


def block_swap(x):
    s = iota((8, 256), 0)
    b = iota((8, 256), 1) // 32
    out = x
    for d in range(1, 8):
        moved = pltpu.roll(pltpu.roll(x, d, 0), 256 - 32 * d, 1)
        out = jnp.where((s - b) % 8 == d, moved, out)
    return out


def build_rows(k, rows):
    rows[...] = jnp.zeros_like(rows)
    m = iota((128, 128), 1)
    b = iota((128, 128), 0)
    for r in range(4):
        pick = ((m == (32 * r - 1 - b + 256) % 128) & (b < 31)).astype(F32)
        moved = jnp.dot(k, pick, precision=HI, preferred_element_type=F32)
        rows[5 + r : 37 + r, :] = rows[5 + r : 37 + r, :] + moved


def build_operator(rows, op_hi, op_lo, start, stop):
    c2 = iota((64, 128), 0)
    b = c2 - 1 - iota((64, 128), 1) % 32
    inside = (b >= 0) & (b <= 30)

    def step(j, carry):
        wide = jnp.broadcast_to(rows[pl.ds(j, 1), :], (64, 128))
        value = jnp.where(inside, pltpu.roll(wide, 0, 1, stride=1, stride_axis=0), 0.0)
        hi = value.astype(BF)
        lo = (value - hi.astype(F32)).astype(BF)
        first = pl.multiple_of(j * 64, 64)
        second = pl.multiple_of(j * 64 + 256, 64)
        op_hi[pl.ds(first, 64), 0:128] = hi
        op_lo[pl.ds(first, 64), 0:128] = lo
        op_hi[pl.ds(second, 64), 128:256] = hi
        op_lo[pl.ds(second, 64), 128:256] = lo
        return carry

    lax.fori_loop(start, stop, step, 0)


def windows(v):
    n = v.shape[0]
    group = iota(v.shape, 0) % 8
    lane = iota(v.shape, 1)
    before = jnp.where(group > 0, pltpu.roll(v, 1, 0), 0.0)
    after = jnp.where(group < 7, pltpu.roll(v, n - 1, 0), 0.0)

    def pair(mid0, left0, right0, mid1, left1, right1):
        out = jnp.where(lane < 16, pltpu.roll(before, left0, 1), pltpu.roll(v, mid0, 1))
        out = jnp.where(lane >= 48, pltpu.roll(after, right0, 1), out)
        out = jnp.where(lane >= 64, pltpu.roll(before, left1, 1), out)
        out = jnp.where(lane >= 80, pltpu.roll(v, mid1, 1), out)
        return jnp.where(lane >= 112, pltpu.roll(after, right1, 1), out)

    return pair(16, 112, 48, 48, 16, 80), pair(80, 48, 112, 112, 80, 16)


def put_windows(value, first_block, wide):
    rows = value.shape[0]
    at = pl.multiple_of(first_block * 8, 8)
    for q in range(2):
        one, two = windows(value[:, 128 * q : 128 * q + 128])
        wide[q, pl.ds(at, rows), 0:128] = one
        wide[q, pl.ds(at, rows), 128:256] = two


def product(wide, m, x_hi, x_lo, op_hi, op_lo):
    for part in range(10):
        value = wide[part % 2, (part // 2) * 8 : (part // 2) * 8 + m, :]
        hi = value.astype(BF)
        x_hi[0:m, 256 * part : 256 * part + 256] = hi
        x_lo[0:m, 256 * part : 256 * part + 256] = (value - hi.astype(F32)).astype(BF)

    def dot(x, op):
        return jnp.dot(x[0:m, :], op[256 : 256 + 2560, :], preferred_element_type=F32)

    return dot(x_hi, op_hi) + (dot(x_hi, op_lo) + dot(x_lo, op_hi))


def kernel(
    exp_ref, sky_ref, ker_ref, cov_ref, out_ref,
    kpad, rows, fwd_hi, fwd_lo, flip_hi, flip_lo, wide, x_hi, x_lo,
    own, prev, follow, exp_prev, exp_follow, expo, ratio, norm,
    q_sum, q_in, nums, r_core, a_sum, r_y, b_sum, r_z,
    ag_send, ag_recv, rs_send, rs_recv, q_send, q_recv, e_send, e_recv,
):
    t = lax.axis_index("tile")
    v = lax.axis_index("visit")
    tiles = lax.axis_size("tile")
    z, y, c = v // 8, (v // 2) % 4, v % 2

    def at_z(z2):
        return {"visit": z2 * 8 + y * 2 + c, "tile": t}

    def at_y(y2):
        return {"visit": z * 8 + y2 * 2 + c, "tile": t}

    partner = {"visit": z * 8 + y * 2 + (1 - c), "tile": t}
    up = {"visit": v, "tile": t + 1}
    down = {"visit": v, "tile": t - 1}
    has_up = t < tiles - 1
    has_down = t > 0

    barrier = pltpu.get_barrier_semaphore()
    peers = [at_z((z + d) % 4) for d in (1, 2, 3)] + [at_y((y + d) % 4) for d in (1, 2, 3)] + [partner]
    for peer in peers:
        pl.semaphore_signal(barrier, inc=1, device_id=peer, device_id_type=MESH)

    @pl.when(has_up)
    def _():
        pl.semaphore_signal(barrier, inc=1, device_id=up, device_id_type=MESH)

    @pl.when(has_down)
    def _():
        pl.semaphore_signal(barrier, inc=1, device_id=down, device_id_type=MESH)

    def remote(src, dst, send, recv, device):
        return pltpu.make_async_remote_copy(
            src_ref=src, dst_ref=dst, send_sem=send, recv_sem=recv, device_id=device, device_id_type=MESH
        )

    prev[...] = jnp.zeros_like(prev)
    follow[...] = jnp.zeros_like(follow)
    kpad[...] = jnp.zeros_like(kpad)
    raw = ker_ref[0]
    kpad[0:31, 0:31] = raw / jnp.sum(raw)
    own[0, z, y, c] = block_swap(sky_ref[...])
    w_here = cov_ref[0, t].astype(F32)
    w_down = jnp.where(has_down, cov_ref[0, jnp.maximum(t - 1, 0)], 0).astype(F32)
    w_up = jnp.where(has_up, cov_ref[0, jnp.minimum(t + 1, tiles - 1)], 0).astype(F32)
    edge = iota((32, 32), 0) + iota((32, 32), 1)
    weights = jnp.where(edge < 15, w_down, jnp.where(edge >= 46, w_up, w_here))
    q_sum[0] = jnp.dot(weights, kpad[...], precision=HI, preferred_element_type=F32)

    turn_rows = (iota((32, 32), 0) + iota((32, 32), 1) == 30).astype(F32)
    turn_cols = (iota((128, 128), 0) + iota((128, 128), 1) == 30).astype(F32)
    turned = jnp.dot(turn_rows, kpad[...], precision=HI, preferred_element_type=F32)
    turned = jnp.dot(turned, turn_cols, precision=HI, preferred_element_type=F32)
    build_rows(turned, rows)
    build_operator(rows, flip_hi, flip_lo, 0, 44)

    count = 7 + has_up.astype(jnp.int32) + has_down.astype(jnp.int32)
    pl.semaphore_wait(barrier, count)

    def send_exposures(act):
        @pl.when(has_up)
        def _():
            act(remote(exp_ref.at[0, 240:256, :], exp_prev, e_send.at[0], e_recv.at[0], up))

        @pl.when(has_down)
        def _():
            act(remote(exp_ref.at[0, 0:16, :], exp_follow, e_send.at[1], e_recv.at[1], down))

    def recv_exposures():
        @pl.when(has_down)
        def _():
            remote(exp_ref.at[0, 240:256, :], exp_prev, e_send.at[0], e_recv.at[0], down).wait_recv()

        @pl.when(has_up)
        def _():
            remote(exp_ref.at[0, 0:16, :], exp_follow, e_send.at[1], e_recv.at[1], up).wait_recv()

    def halo_up(it, device):
        return remote(own.at[it, 3, 2:4], prev.at[it], ag_send.at[it, 7], ag_recv.at[it, 7], device)

    def halo_down(it, device):
        return remote(own.at[it, 0, 0:2], follow.at[it], ag_send.at[it, 8], ag_recv.at[it, 8], device)

    def send_halo(it, act):
        @pl.when(has_up)
        def _():
            act(halo_up(it, up))

        @pl.when(has_down)
        def _():
            act(halo_down(it, down))

    def recv_halo(it):
        @pl.when(has_down)
        def _():
            halo_up(it, down).wait_recv()

        @pl.when(has_up)
        def _():
            halo_down(it, up).wait_recv()

    pending = []

    def start(copies):
        for copy in copies:
            copy.start()
        pending.extend(copies)
        return copies

    def gather_z(it):
        part = own.at[it, z, y, c]
        return [remote(part, part, ag_send.at[it, d - 1], ag_recv.at[it, d - 1], at_z((z + d) % 4)) for d in (1, 2, 3)]

    def gather_y(it):
        part = own.at[it, :, y, c]
        return [remote(part, part, ag_send.at[it, d + 2], ag_recv.at[it, d + 2], at_y((y + d) % 4)) for d in (1, 2, 3)]

    def gather_core(it):
        part = own.at[it, :, :, c]
        return [remote(part, part, ag_send.at[it, 6], ag_recv.at[it, 6], partner)]

    def q_copies(stage, devices, base):
        return [
            remote(q_sum.at[stage], q_in.at[base + i], q_send.at[base + i], q_recv.at[base + i], device)
            for i, device in enumerate(devices)
        ]

    def arrive(copies):
        for copy in copies:
            copy.wait_recv()

    stage = start(gather_z(0) + q_copies(0, [at_z((z + d) % 4) for d in (1, 2, 3)], 0))
    send_exposures(lambda copy: copy.start())
    build_rows(kpad[...], rows)
    build_operator(rows, fwd_hi, fwd_lo, 0, 30)
    arrive(stage)
    q_sum[1] = q_sum[0] + q_in[0] + q_in[1] + q_in[2]
    stage = start(gather_y(0) + q_copies(1, [at_y((y + d) % 4) for d in (1, 2, 3)], 3))
    build_operator(rows, fwd_hi, fwd_lo, 30, 44)

    def swap_exposure(i, carry):
        for j in range(4):
            first = pl.multiple_of(32 * i + 8 * j, 8)
            expo[4 * i + j + 2] = block_swap(exp_ref[0, pl.ds(first, 8), :])
        return carry

    lax.fori_loop(0, 8, swap_exposure, 0)
    arrive(stage)
    q_sum[2] = q_sum[1] + q_in[3] + q_in[4] + q_in[5]
    stage = start(gather_core(0) + q_copies(2, [partner], 6))
    recv_exposures()
    for i in range(2):
        expo[i] = block_swap(exp_prev[8 * i : 8 * i + 8, :])
        expo[34 + i] = block_swap(exp_follow[8 * i : 8 * i + 8, :])
    arrive(stage)

    for it in range(ITERS):
        if it > 0:
            stage = start(gather_z(it))
            arrive(stage)
            stage = start(gather_y(it))
            arrive(stage)
            stage = start(gather_core(it))
            arrive(stage)
        send_halo(it, lambda copy: copy.start())
        if it == 0:
            q_sum[3] = q_sum[2] + q_in[6]
            lines = []
            for s in range(8):
                r = 8 * v + s
                line = jnp.where(r < 15, r, jnp.where(r > 240, r - 225, 15))
                lines.append(q_sum[3, pl.ds(line, 1), :])
            cover = iota((128, 256), 1) + iota((128, 256), 0) - 15
            valid = ((cover >= 0) & (cover < 256) & (iota((128, 256), 0) < 31)).astype(F32)
            field = jnp.dot(jnp.concatenate(lines, axis=0), valid, precision=HI, preferred_element_type=F32)
            norm[...] = block_swap(field)

        def own_windows(i, carry, it=it):
            zz, yy = i // 2, (i % 2) * 2
            put_windows(own[it, zz, pl.ds(yy, 2)].reshape(32, 256), 4 + 4 * i, wide)
            return carry

        lax.fori_loop(0, 8, own_windows, 0)
        recv_halo(it)
        put_windows(prev[it].reshape(32, 256), 0, wide)
        put_windows(follow[it].reshape(32, 256), 36, wide)
        blurred = product(wide, 288, x_hi, x_lo, flip_hi, flip_lo)

        for i, (low, high, weight, there) in enumerate(
            ((0, 2, w_down, has_down), (2, 34, w_here, None), (34, 36, w_up, has_up))
        ):
            part = weight * expo[low:high].reshape((high - low) * 8, 256) / blurred[low * 8 : high * 8]
            if there is not None:
                part = jnp.where(there, part, 0.0)
            ratio[low:high] = part.reshape(high - low, 8, 256)

        def ratio_windows(i, carry):
            put_windows(ratio[pl.ds(4 * i, 4)].reshape(32, 256), 4 * i, wide)
            return carry

        lax.fori_loop(0, 9, ratio_windows, 0)
        nums[it] = product(wide, 256, x_hi, x_lo, fwd_hi, fwd_lo).reshape(4, 4, 2, 8, 256)

        stage = start([remote(nums.at[it, :, :, 1 - c], r_core.at[it], rs_send.at[it, 0], rs_recv.at[it, 0], partner)])
        arrive(stage)
        a_sum[it] = nums[it, :, :, c] + r_core[it]
        stage = start(
            [
                remote(
                    a_sum.at[it, :, (y + d) % 4], r_y.at[it, d - 1],
                    rs_send.at[it, d], rs_recv.at[it, d], at_y((y + d) % 4),
                )
                for d in (1, 2, 3)
            ]
        )
        arrive(stage)
        b_sum[it] = a_sum[it, :, y] + r_y[it, 0] + r_y[it, 1] + r_y[it, 2]
        stage = start(
            [
                remote(
                    b_sum.at[it, (z + d) % 4], r_z.at[it, d - 1],
                    rs_send.at[it, d + 3], rs_recv.at[it, d + 3], at_z((z + d) % 4),
                )
                for d in (1, 2, 3)
            ]
        )
        arrive(stage)
        total = b_sum[it, z] + r_z[it, 0] + r_z[it, 1] + r_z[it, 2]
        model = own[it, z, y, c] * total / norm[...]
        if it < ITERS - 1:
            own[it + 1, z, y, c] = model
        else:
            out_ref[...] = block_swap(model)

    for copy in pending:
        copy.wait_send()
    send_exposures(lambda copy: copy.wait_send())
    for it in range(ITERS):
        send_halo(it, lambda copy: copy.wait_send())


def body(exposures, sky_model, blur_kernels, coverage):
    vmem = pl.BlockSpec(memory_space=pltpu.VMEM)
    V = pltpu.VMEM
    D = pltpu.SemaphoreType.DMA
    return pl.pallas_call(
        kernel,
        out_shape=jax.ShapeDtypeStruct((8, 256), F32),
        in_specs=[vmem, vmem, vmem, pl.BlockSpec(memory_space=pltpu.SMEM)],
        out_specs=vmem,
        scratch_shapes=[
            V((32, 128), F32), V((48, 128), F32),
            V((3072, 256), BF), V((3072, 256), BF), V((3072, 256), BF), V((3072, 256), BF),
            V((2, 320, 256), F32), V((288, 2560), BF), V((288, 2560), BF),
            V((2, 4, 4, 2, 8, 256), F32), V((2, 2, 2, 8, 256), F32), V((2, 2, 2, 8, 256), F32),
            V((16, 256), F32), V((16, 256), F32), V((36, 8, 256), F32), V((36, 8, 256), F32), V((8, 256), F32),
            V((4, 32, 128), F32), V((7, 32, 128), F32),
            V((2, 4, 4, 2, 8, 256), F32), V((2, 4, 4, 8, 256), F32), V((2, 4, 4, 8, 256), F32),
            V((2, 3, 4, 8, 256), F32), V((2, 4, 8, 256), F32), V((2, 3, 8, 256), F32),
            D((2, 9)), D((2, 9)), D((2, 7)), D((2, 7)), D((7,)), D((7,)), D((2,)), D((2,)),
        ],
        compiler_params=pltpu.CompilerParams(collective_id=0, has_side_effects=True),
    )(exposures, sky_model, blur_kernels, coverage)


def solution(mesh):
    return jax.shard_map(
        body,
        mesh=mesh,
        in_specs=(
            P("visit", "tile", None),
            P(("tile", "visit"), None),
            P("visit", None, None),
            P("visit", None),
        ),
        out_specs=P(("tile", "visit"), None),
        check_vma=False,
    )
```

time: 644 us -> 72.3 us (0.11)
  waiting for transfers between devices: 424 us -> 0 us
  blocking collectives: 83.8 us -> 0 us
  Pallas kernels: 0 us -> 69.5 us
  matrix products: 59.2 us -> 0 us
  starting transfers between devices: 32.8 us -> 0 us
  local copies, waits for them, and re-layouts: 20.3 us -> 2.61 us
  between operations: 13.3 us -> 0.01 us
  other arithmetic: 9.28 us -> 0 us
    reduce_scatter x3 -> x0, waiting for transfers between devices: 407 us -> none  [the longest x2 285 us: body(): lax.psum_scatter(numerator, 'visit', scatter_dimension=0, tiled=True)]
    all_gather x2 -> x0, blocking collectives: 83.8 us -> none  [body(): whole = lax.all_gather(model_shard, 'visit', axis=0, tiled=True)]
    pallas_call x0 -> x1, Pallas kernels: none -> 69.5 us  [body(): pl.pallas_call(kernel, out_shape=jax.ShapeDtypeStruct((8, 256), F32), in_...]
    dot_general x8 -> x0, matrix products: 59.2 us -> none  [the longest x4 44.8 us: correlate(): product = jnp.dot(extended, operator, precision=lax.Precision.HIGHEST)]
    ppermute x8 -> x0, starting transfers between devices: 32.6 us -> none  [the longest x4 22.7 us: padded(): before = lax.ppermute(last, axis, up)]
    transpose x2 -> x0, local copies, waits for them, and re-layouts: 19.9 us -> none  [column_operator(): operator = operator.reshape(width, width, kernel_len).transpose(0, 2, 1)]
    ppermute x8 -> x0, waiting for transfers between devices: 17.2 us -> none  [the longest x4 17.2 us: padded(): after = lax.ppermute(initial, axis, down)]
  transfers between devices with their start and end apart: 11 -> 0, of which waited for: 5 -> 0; matrix products, arithmetic and copies ran while one was open for 8% -> 0% of each run, Pallas kernels for 0% -> 0%
where the time goes in v1:
time: 72.3 us; the launch traced here: 72.1 us
  Pallas kernels  69.5 us (96%)
  local copies, waits for them, and re-layouts  2.61 us (4%)
    pallas_call x1, Pallas kernels, body(): pl.pallas_call(kernel, out_shape=jax.ShapeDtypeStruct((8, 256), F32), in_...  69.5 us
    unnamed x2, local copies, waits for them, and re-layouts  2.61 us

profile of v1, /device:TPU:6, one launch (start us, length us, event | category | flops | bytes accessed | tf_op | source)
XLA Modules:
  0.0 72.1 jit_solution(1793361721762187566)
XLA Ops:
  0.0 1.3 %copy.5.ker_ref = f32[1,31,31]{2,1,0:T(8,128)} copy(f32[1,31,31]{2,0,1:T(1,128)} %param.6) | data formatting | bytes 7688 | tf_op args[2]
  1.3 69.5 %shard_map.46 = f32[8,256]{1,0:T(8,128)} custom-call(f32[1,256,256]{2,1,0:T(8,128)} %exp_ref.1, f32[8,256]{1,0:T(8,128)} %sky_ref.1, f32[1,31,31]{2,1,0:T(8,128)} %copy.5.ker_ref, s32[1,8]{1,0:T(1,128)} %cov_ref.1), custom_call_target="tpu_custom_call" | custom-call | tf_op jit(solution)/shard_map/pallas_call | solution.py:350
  70.8 1.3 %copy.7 = f32[8,256]{1,0:T(8,128)} copy(f32[8,256]{1,0:T(8,128)} %shard_map.46) | data formatting | bytes 16384

commit v2 on v0

v2 whole, which is shorter than its diff:
```python
import jax
import jax.numpy as jnp
from jax import lax
from jax.experimental import pallas as pl
from jax.experimental.pallas import tpu as pltpu
from jax.sharding import PartitionSpec as P

F32 = jnp.float32
BF = jnp.bfloat16
HI = lax.Precision.HIGHEST
MESH = pl.DeviceIdType.MESH
ITERS = 2


def iota(shape, dim):
    return lax.broadcasted_iota(jnp.int32, shape, dim)


def block_swap(x):
    s = iota((8, 256), 0)
    b = iota((8, 256), 1) // 32
    out = x
    for d in range(1, 8):
        moved = pltpu.roll(pltpu.roll(x, d, 0), 256 - 32 * d, 1)
        out = jnp.where((s - b) % 8 == d, moved, out)
    return out


def build_rows(k, rows):
    rows[...] = jnp.zeros_like(rows)
    m = iota((128, 128), 1)
    b = iota((128, 128), 0)
    for r in range(4):
        pick = ((m == (32 * r - 1 - b + 256) % 128) & (b < 31)).astype(F32)
        moved = jnp.dot(k, pick, precision=HI, preferred_element_type=F32)
        rows[5 + r : 37 + r, :] = rows[5 + r : 37 + r, :] + moved


def build_operator(rows, op_hi, op_lo):
    c2 = iota((64, 128), 0)
    b = c2 - 1 - iota((64, 128), 1) % 32
    inside = (b >= 0) & (b <= 30)

    def step(j, carry):
        wide = jnp.broadcast_to(rows[pl.ds(j, 1), :], (8, 128))
        base = pltpu.roll(wide, 0, 1, stride=1, stride_axis=0)
        value = jnp.concatenate([base] + [pltpu.roll(base, 8 * i, 1) for i in range(1, 8)], axis=0)
        value = jnp.where(inside, value, 0.0)
        hi = value.astype(BF)
        lo = (value - hi.astype(F32)).astype(BF)
        for shift, lanes in ((4, slice(0, 128)), (8, slice(128, 256))):
            o, r = (j + shift) // 8, (j + shift) % 8
            for op, x in ((op_hi, hi), (op_lo, lo)):
                op[o, 0, r, :, lanes] = x[16:48]
                op[o, 1, r, 0:16, lanes] = x[48:64]
                op[o, 1, r, 16:32, lanes] = x[0:16]
        return carry

    lax.fori_loop(0, 44, step, 0, unroll=11)


def put_near(value, first, near):
    n = value.shape[0]
    group = iota(value.shape, 0) % 8
    before = jnp.where(group > 0, pltpu.roll(value, 1, 0), 0.0)
    after = jnp.where(group < 7, pltpu.roll(value, n - 1, 0), 0.0)
    near[first : first + n, :] = jnp.where(iota(value.shape, 1) % 32 < 16, after, before)


def product(mid, near, ranges, x_hi, x_lo, op_hi, op_lo):
    row = 0
    for first, count in ranges:
        m = 8 * count
        for o in range(5):
            for k, src in ((0, mid), (1, near)):
                value = src[(first + o) * 8 : (first + o) * 8 + m, :]
                hi = value.astype(BF)
                at = 512 * o + 256 * k
                x_hi[row : row + m, at : at + 256] = hi
                x_lo[row : row + m, at : at + 256] = (value - hi.astype(F32)).astype(BF)
        row += m

    def dot(x, op):
        return jnp.dot(x[0:row, :], op[1:6].reshape(2560, 256), preferred_element_type=F32)

    return dot(x_hi, op_hi) + (dot(x_hi, op_lo) + dot(x_lo, op_hi))


def far(d):
    return -(d[0] + (2 if d[1] == 2 else 1 if d[1] else 0))


AWAY = sorted([(dz, dy) for dz in range(4) for dy in range(4) if (dz, dy) != (0, 0)], key=far)


def kernel(
    exp_hbm, sky_ref, ker_ref, cov_ref, out_ref,
    exp_ref, kpad, rows, fwd_hi, fwd_lo, flip_hi, flip_lo, mid, near, rmid, rnear, x_hi, x_lo,
    own, prev, follow, exp_prev, exp_follow, expo,
    q_all, q_core, q_sum, q_in, nums, r_core, a_sum, r_in,
    exp_sem, ag_send, ag_recv, cf_send, cf_recv, hx_send, hx_recv, hr_send, hr_recv, hc_send, hc_recv,
    rc_send, rc_recv, rs_send, rs_recv, q_send, q_recv, e_send, e_recv,
):
    t = lax.axis_index("tile")
    v = lax.axis_index("visit")
    tiles = lax.axis_size("tile")
    z, y, c = v // 8, (v // 2) % 4, v % 2
    u = v // 2

    def there(d):
        return {"visit": ((z + d[0]) % 4) * 8 + ((y + d[1]) % 4) * 2 + c, "tile": t}

    partner = {"visit": 2 * u + (1 - c), "tile": t}
    up = {"visit": v, "tile": t + 1}
    down = {"visit": v, "tile": t - 1}
    has_up = t < tiles - 1
    has_down = t > 0

    prev[...] = jnp.zeros_like(prev)
    follow[...] = jnp.zeros_like(follow)
    barrier = pltpu.get_barrier_semaphore()
    for peer in [there(d) for d in AWAY] + [partner]:
        pl.semaphore_signal(barrier, inc=1, device_id=peer, device_id_type=MESH)

    @pl.when(has_up)
    def _():
        pl.semaphore_signal(barrier, inc=1, device_id=up, device_id_type=MESH)

    @pl.when(has_down)
    def _():
        pl.semaphore_signal(barrier, inc=1, device_id=down, device_id_type=MESH)

    load = pltpu.make_async_copy(exp_hbm.at[0], exp_ref, exp_sem)
    load.start()

    def remote(src, dst, send, recv, device):
        return pltpu.make_async_remote_copy(
            src_ref=src, dst_ref=dst, send_sem=send, recv_sem=recv, device_id=device, device_id_type=MESH
        )

    sent = []

    def start(copies):
        for copy in copies:
            copy.start()
        sent.extend(copies)
        return copies

    def arrive(copies):
        for copy in copies:
            copy.wait_recv()

    def when(cond, act):
        pl.when(cond)(act)

    own[0, u, c] = block_swap(sky_ref[...])
    kpad[...] = jnp.zeros_like(kpad)
    raw = ker_ref[:, 0, :]
    kpad[0:31, 0:31] = raw / jnp.sum(raw)
    w_here = cov_ref[0, t].astype(F32)
    w_down = jnp.where(has_down, cov_ref[0, jnp.maximum(t - 1, 0)], 0).astype(F32)
    w_up = jnp.where(has_up, cov_ref[0, jnp.minimum(t + 1, tiles - 1)], 0).astype(F32)
    edge = iota((32, 32), 0) + iota((32, 32), 1)
    weights = jnp.where(edge < 15, w_down, jnp.where(edge >= 46, w_up, w_here))
    lines = jnp.dot(weights, kpad[...], precision=HI, preferred_element_type=F32)
    for owner in range(32):
        if owner < 2:
            piece = lines[8 * owner : 8 * owner + 8]
        elif owner >= 30:
            piece = lines[8 * owner - 225 : 8 * owner - 217]
        else:
            piece = jnp.broadcast_to(lines[15:16], (8, 128))
        q_all[owner // 2, owner % 2] = piece

    pl.semaphore_wait(barrier, 16 + has_up.astype(jnp.int32) + has_down.astype(jnp.int32))

    def edge_up(device):
        return remote(exp_ref.at[240:256, :], exp_prev, e_send.at[0], e_recv.at[0], device)

    def edge_down(device):
        return remote(exp_ref.at[0:16, :], exp_follow, e_send.at[1], e_recv.at[1], device)

    def hop_up(it, device):
        return remote(own.at[it, u, c], prev.at[it, u % 2, c], hx_send.at[it, 0], hx_recv.at[it, 0], device)

    def hop_down(it, device):
        return remote(own.at[it, u, c], follow.at[it, u % 2, c], hx_send.at[it, 1], hx_recv.at[it, 1], device)

    last = u >= 14
    first = u < 2

    def relay(it, which):
        buf = (prev, follow)[which].at[it, u % 2, c]
        recv = hr_recv.at[it, which, u % 2]
        return [remote(buf, buf, hr_send.at[it, which, i], recv, there(d)) for i, d in enumerate(AWAY)]

    def relayed(it, which, j):
        buf = (prev, follow)[which].at[it, j, c]
        return remote(buf, buf, hr_send.at[it, which, 0], hr_recv.at[it, which, j], partner)

    def pass_halo(it, which):
        buf = (prev, follow)[which].at[it, :, c]
        return remote(buf, buf, hc_send.at[it, which], hc_recv.at[it, which], partner)

    for it in range(ITERS):
        mine = own.at[it, u, c]
        when(last & has_up, lambda: hop_up(it, up).start())
        when(first & has_down, lambda: hop_down(it, down).start())
        gather = start(
            [remote(mine, mine, ag_send.at[it, i], ag_recv.at[it, i], there(d)) for i, d in enumerate(AWAY)]
        )
        if it == 0:
            q_swap = start([remote(q_all.at[:, 1 - c], q_core, q_send.at[15], q_recv.at[15], partner)])
            load.wait()
            when(has_up, lambda: edge_up(up).start())
            when(has_down, lambda: edge_down(down).start())
            turn_rows = (iota((32, 32), 0) + iota((32, 32), 1) == 30).astype(F32)
            turn_cols = (iota((128, 128), 0) + iota((128, 128), 1) == 30).astype(F32)
            turned = jnp.dot(turn_rows, kpad[...], precision=HI, preferred_element_type=F32)
            turned = jnp.dot(turned, turn_cols, precision=HI, preferred_element_type=F32)
            build_rows(turned, rows)
            build_operator(rows, flip_hi, flip_lo)

        def relay_up():
            hop_up(it, down).wait_recv()
            for copy in relay(it, 0):
                copy.start()

        def relay_down():
            hop_down(it, up).wait_recv()
            for copy in relay(it, 1):
                copy.start()

        when(last & has_down, relay_up)
        when(first & has_up, relay_down)
        if it == 0:
            build_rows(kpad[...], rows)
            build_operator(rows, fwd_hi, fwd_lo)

            def swap_exposure(i, carry):
                for j in range(4):
                    at = pl.multiple_of(32 * i + 8 * j, 8)
                    expo[4 * i + j + 2] = block_swap(exp_ref[pl.ds(at, 8), :])
                return carry

            lax.fori_loop(0, 8, swap_exposure, 0)

        handed = []
        for dz in range(4):
            for i, d in enumerate(AWAY):
                if d[0] == dz:
                    gather[i].wait_recv()
            part = own.at[it, pl.ds(((z - dz) % 4) * 4, 4), c]
            handed += start([remote(part, part, cf_send.at[it, dz], cf_recv.at[it, dz], partner)])
        if it == 0:
            arrive(q_swap)
            q_sum[...] = q_all[:, c] + q_core[...]
            q_spread = start(
                [
                    remote(
                        q_sum.at[((z + d[0]) % 4) * 4 + (y + d[1]) % 4], q_in.at[i], q_send.at[i], q_recv.at[i], there(d)
                    )
                    for i, d in enumerate(AWAY)
                ]
            )
        arrive(handed)

        for g in range(4):
            value = own[it, 4 * g : 4 * g + 4].reshape(64, 256)
            mid[32 + 64 * g : 96 + 64 * g, :] = value
            put_near(value, 32 + 64 * g, near)
        blurred = product(mid, near, ((4, 28),), x_hi, x_lo, flip_hi, flip_lo)
        value = w_here * expo[4:32].reshape(224, 256) / blurred
        rmid[32:256, :] = value
        for g in range(7):
            put_near(value[32 * g : 32 * g + 32], 32 + 32 * g, rnear)

        for which, comes, relayer in ((0, has_down, last), (1, has_up, first)):
            for j in range(2):
                when(
                    comes & jnp.logical_not(relayer & (u % 2 == j)),
                    lambda which=which, j=j: relayed(it, which, j).wait_recv(),
                )
            when(comes, lambda which=which: pass_halo(it, which).start())

        found = product(rmid, rnear, ((4, 24),), x_hi, x_lo, fwd_hi, fwd_lo)
        nums[it, 2:14] = found.reshape(12, 2, 8, 256)
        swap = start([remote(nums.at[it, 2:14, 1 - c], r_core.at[it, 2:14], rc_send.at[it, 0], rc_recv.at[it, 0], partner)])

        if it == 0:
            when(has_down, lambda: edge_up(down).wait_recv())
            when(has_up, lambda: edge_down(up).wait_recv())
            for i in range(2):
                expo[i] = block_swap(exp_prev[8 * i : 8 * i + 8, :])
                expo[34 + i] = block_swap(exp_follow[8 * i : 8 * i + 8, :])
        when(has_down, lambda: pass_halo(it, 0).wait_recv())
        when(has_up, lambda: pass_halo(it, 1).wait_recv())
        for buf, at in ((prev, 0), (follow, 288)):
            value = buf[it].reshape(32, 256)
            mid[at : at + 32, :] = value
            put_near(value, at, near)
        blurred = product(mid, near, ((0, 4), (32, 4)), x_hi, x_lo, flip_hi, flip_lo)
        for low, source, count, weight, comes in (
            (0, 0, 2, w_down, has_down),
            (2, 16, 2, w_here, None),
            (32, 32, 2, w_here, None),
            (34, 48, 2, w_up, has_up),
        ):
            value = weight * expo[low : low + count].reshape(16, 256) / blurred[source : source + 16]
            if comes is not None:
                value = jnp.where(comes, value, 0.0)
            rmid[8 * low : 8 * low + 16, :] = value
            put_near(value, 8 * low, rnear)

        arrive(swap)
        a_sum[it, 2:14] = nums[it, 2:14, c] + r_core[it, 2:14]

        def owners(d):
            return ((z + d[0]) % 4) * 4 + (y + d[1]) % 4

        def at_edge(place):
            return (place < 2) | (place >= 14)

        spread = [
            remote(a_sum.at[it, owners(d)], r_in.at[it, i], rs_send.at[it, i], rs_recv.at[it, i], there(d))
            for i, d in enumerate(AWAY)
        ]
        for d, copy in zip(AWAY, spread):
            when(jnp.logical_not(at_edge(owners(d))), copy.start)

        found = product(rmid, rnear, ((0, 4), (28, 4)), x_hi, x_lo, fwd_hi, fwd_lo)
        nums[it, 0:2] = found[0:32].reshape(2, 2, 8, 256)
        nums[it, 14:16] = found[32:64].reshape(2, 2, 8, 256)
        swap = start(
            [
                remote(nums.at[it, at : at + 2, 1 - c], r_core.at[it, at : at + 2], rc_send.at[it, k], rc_recv.at[it, k], partner)
                for k, at in ((1, 0), (2, 14))
            ]
        )
        arrive(swap)
        for at in (0, 14):
            a_sum[it, at : at + 2] = nums[it, at : at + 2, c] + r_core[it, at : at + 2]
        for d, copy in zip(AWAY, spread):
            when(at_edge(owners(d)), copy.start)
        sent.extend(spread)

        if it == 0:
            arrive(q_spread)
            line = q_sum[u]
            for i in range(15):
                line = line + q_in[i]
            cover = iota((128, 256), 1) + iota((128, 256), 0) - 15
            valid = ((cover >= 0) & (cover < 256) & (iota((128, 256), 0) < 31)).astype(F32)
            norm = block_swap(jnp.dot(line, valid, precision=HI, preferred_element_type=F32))

        arrive(spread)
        total = a_sum[it, u]
        for i in range(15):
            total = total + r_in[it, i]
        model = own[it, u, c] * total / norm
        if it < ITERS - 1:
            own[it + 1, u, c] = model
        else:
            out_ref[...] = block_swap(model)

    for copy in sent:
        copy.wait_send()
    when(has_up, lambda: edge_up(up).wait_send())
    when(has_down, lambda: edge_down(down).wait_send())
    for it in range(ITERS):
        when(last & has_up, lambda: hop_up(it, up).wait_send())
        when(first & has_down, lambda: hop_down(it, down).wait_send())
        for which, comes, relayer in ((0, has_down, last), (1, has_up, first)):

            def drain(which=which):
                for copy in relay(it, which):
                    copy.wait_send()

            when(comes & relayer, drain)
            when(comes, lambda which=which: pass_halo(it, which).wait_send())


def body(exposures, sky_model, blur_kernels, coverage):
    vmem = pl.BlockSpec(memory_space=pltpu.VMEM)
    V = pltpu.VMEM
    D = pltpu.SemaphoreType.DMA
    op = V((7, 2, 8, 32, 256), BF)
    return pl.pallas_call(
        kernel,
        out_shape=jax.ShapeDtypeStruct((8, 256), F32),
        in_specs=[pl.BlockSpec(memory_space=pl.ANY), vmem, vmem, pl.BlockSpec(memory_space=pltpu.SMEM)],
        out_specs=vmem,
        scratch_shapes=[
            V((256, 256), F32), V((32, 128), F32), V((48, 128), F32), op, op, op, op,
            V((320, 256), F32), V((320, 256), F32), V((288, 256), F32), V((288, 256), F32),
            V((224, 2560), BF), V((224, 2560), BF),
            V((2, 16, 2, 8, 256), F32), V((2, 2, 2, 8, 256), F32), V((2, 2, 2, 8, 256), F32),
            V((16, 256), F32), V((16, 256), F32), V((36, 8, 256), F32),
            V((16, 2, 8, 128), F32), V((16, 8, 128), F32), V((16, 8, 128), F32), V((15, 8, 128), F32),
            V((2, 16, 2, 8, 256), F32), V((2, 16, 8, 256), F32), V((2, 16, 8, 256), F32), V((2, 15, 8, 256), F32),
            D, D((2, 15)), D((2, 15)), D((2, 4)), D((2, 4)), D((2, 2)), D((2, 2)), D((2, 2, 15)), D((2, 2, 2)),
            D((2, 2)), D((2, 2)), D((2, 3)), D((2, 3)), D((2, 15)), D((2, 15)), D((16,)), D((16,)), D((2,)), D((2,)),
        ],
        compiler_params=pltpu.CompilerParams(collective_id=0, has_side_effects=True),
    )(exposures, sky_model, jnp.transpose(blur_kernels, (1, 0, 2)), coverage)


def solution(mesh):
    return jax.shard_map(
        body,
        mesh=mesh,
        in_specs=(
            P("visit", "tile", None),
            P(("tile", "visit"), None),
            P("visit", None, None),
            P("visit", None),
        ),
        out_specs=P(("tile", "visit"), None),
        check_vma=False,
    )
```

time: 644 us -> 55.9 us (0.09)
  waiting for transfers between devices: 424 us -> 0 us
  blocking collectives: 83.8 us -> 0 us
  matrix products: 59.2 us -> 0 us
  Pallas kernels: 0 us -> 54.3 us
  starting transfers between devices: 32.8 us -> 0 us
  local copies, waits for them, and re-layouts: 20.3 us -> 1.3 us
  between operations: 13.3 us -> 0.01 us
  other arithmetic: 9.28 us -> 0 us
    reduce_scatter x3 -> x0, waiting for transfers between devices: 407 us -> none  [the longest x2 285 us: body(): lax.psum_scatter(numerator, 'visit', scatter_dimension=0, tiled=True)]
    all_gather x2 -> x0, blocking collectives: 83.8 us -> none  [body(): whole = lax.all_gather(model_shard, 'visit', axis=0, tiled=True)]
    dot_general x8 -> x0, matrix products: 59.2 us -> none  [the longest x4 44.8 us: correlate(): product = jnp.dot(extended, operator, precision=lax.Precision.HIGHEST)]
    pallas_call x0 -> x1, Pallas kernels: none -> 54.3 us  [body(): pl.pallas_call(kernel, out_shape=jax.ShapeDtypeStruct((8, 256), F32), in_...]
    ppermute x8 -> x0, starting transfers between devices: 32.6 us -> none  [the longest x4 22.7 us: padded(): before = lax.ppermute(last, axis, up)]
    transpose x2 -> x0, local copies, waits for them, and re-layouts: 19.9 us -> none  [column_operator(): operator = operator.reshape(width, width, kernel_len).transpose(0, 2, 1)]
    ppermute x8 -> x0, waiting for transfers between devices: 17.2 us -> none  [the longest x4 17.2 us: padded(): after = lax.ppermute(initial, axis, down)]
  transfers between devices with their start and end apart: 11 -> 0, of which waited for: 5 -> 0; matrix products, arithmetic and copies ran while one was open for 8% -> 0% of each run, Pallas kernels for 0% -> 0%
where the time goes in v2:
time: 55.9 us; the launch traced here: 55.6 us
  Pallas kernels  54.3 us (97%)
  local copies, waits for them, and re-layouts  1.3 us (2%)
    pallas_call x1, Pallas kernels, body(): pl.pallas_call(kernel, out_shape=jax.ShapeDtypeStruct((8, 256), F32), in_...  54.3 us
    unnamed x1, local copies, waits for them, and re-layouts  1.3 us

profile of v2, /device:TPU:6, one launch (start us, length us, event | category | flops | bytes accessed | tf_op | source)
XLA Modules:
  0.0 55.6 jit_solution(17915545261025060046)
XLA Ops:
  0.0 54.3 %shard_map.46 = f32[8,256]{1,0:T(8,128)} custom-call(f32[1,256,256]{2,1,0:T(8,128)} %exp_hbm.1, f32[8,256]{1,0:T(8,128)} %sky_ref.1, f32[31,1,31]{2,1,0:T(1,128)} %bitcast.1, s32[1,8]{1,0:T(1,128)} %cov_ref.1), custom_call_target="tpu_custom_call" | custom-call | tf_op jit(solution)/shard_map/pallas_call | solution.py:388
  54.3 1.3 %copy.6 = f32[8,256]{1,0:T(8,128)} copy(f32[8,256]{1,0:T(8,128)} %shard_map.46) | data formatting | bytes 16384

commit v3 on v0

v3 whole, which is shorter than its diff:
```python
import jax
import jax.numpy as jnp
from jax import lax
from jax.experimental import pallas as pl
from jax.experimental.pallas import tpu as pltpu
from jax.sharding import PartitionSpec as P

F32 = jnp.float32
BF = jnp.bfloat16
HI = lax.Precision.HIGHEST
MESH = pl.DeviceIdType.MESH
ITERS = 2


def iota(shape, dim):
    return lax.broadcasted_iota(jnp.int32, shape, dim)


def block_swap(x):
    s = iota((8, 256), 0)
    b = iota((8, 256), 1) // 32
    out = x
    for d in range(1, 8):
        moved = pltpu.roll(pltpu.roll(x, d, 0), 256 - 32 * d, 1)
        out = jnp.where((s - b) % 8 == d, moved, out)
    return out


def build_rows(k, rows):
    rows[...] = jnp.zeros_like(rows)
    m = iota((128, 128), 1)
    b = iota((128, 128), 0)
    for r in range(4):
        pick = ((m == (32 * r - 1 - b + 256) % 128) & (b < 31)).astype(F32)
        moved = jnp.dot(k, pick, precision=HI, preferred_element_type=F32)
        rows[5 + r : 37 + r, :] = rows[5 + r : 37 + r, :] + moved


def build_operator(rows, op_hi, op_lo):
    c2 = iota((64, 128), 0)
    b = c2 - 1 - iota((64, 128), 1) % 32
    inside = (b >= 0) & (b <= 30)

    def step(j, carry):
        wide = jnp.broadcast_to(rows[pl.ds(j, 1), :], (8, 128))
        base = pltpu.roll(wide, 0, 1, stride=1, stride_axis=0)
        value = jnp.concatenate([base] + [pltpu.roll(base, 8 * i, 1) for i in range(1, 8)], axis=0)
        value = jnp.where(inside, value, 0.0)
        hi = value.astype(BF)
        lo = (value - hi.astype(F32)).astype(BF)
        for shift, lanes in ((4, slice(0, 128)), (8, slice(128, 256))):
            o, r = (j + shift) // 8, (j + shift) % 8
            for op, x in ((op_hi, hi), (op_lo, lo)):
                op[o, 0, r, :, lanes] = x[16:48]
                op[o, 1, r, 0:16, lanes] = x[48:64]
                op[o, 1, r, 16:32, lanes] = x[0:16]
        return carry

    lax.fori_loop(0, 44, step, 0, unroll=11)


def beside(value):
    n = value.shape[0]
    group = iota(value.shape, 0) % 8
    before = jnp.where(group > 0, pltpu.roll(value, 1, 0), 0.0)
    after = jnp.where(group < 7, pltpu.roll(value, n - 1, 0), 0.0)
    return jnp.where(iota(value.shape, 1) % 32 < 16, after, before)


def put(value, first, mid, near):
    n = value.shape[0]
    mid[first : first + n, :] = value
    near[first : first + n, :] = beside(value)


def weave(ref, first, count):
    pairs = [ref[0, first : first + count], ref[1, first : first + count]]
    return jnp.stack(pairs, axis=1).reshape(16 * count, 256)


def encode(value, code, rows, lanes):
    hi = value.astype(BF)
    code[0, rows, lanes] = hi
    code[1, rows, lanes] = (value - hi.astype(F32)).astype(BF)


def encode_rows(mid, near, code, shift, first, last):
    for at in range(first, last, 64):
        n = min(64, last - at)
        for k, src in ((0, mid), (1, near)):
            rows = slice(at + 8 * shift, at + 8 * shift + n)
            encode(src[rows, :], code.at[shift], slice(at, at + n), slice(256 * k, 256 * k + 256))


def multiply(left, op_hi, op_lo):
    def dot(x, op):
        return jnp.dot(x, op[1:6].reshape(2560, 256), preferred_element_type=F32)

    hi, lo = left
    return dot(hi, op_hi) + (dot(hi, op_lo) + dot(lo, op_hi))


def product(code, ranges, op_hi, op_lo):
    left = []
    for term in range(2):
        parts = []
        for first, count in ranges:
            at = [8 * first + 16 * (o // 2) for o in range(5)]
            parts.append(
                jnp.concatenate([code[o % 2, term, at[o] : at[o] + 8 * count, :] for o in range(5)], axis=1)
            )
        left.append(jnp.concatenate(parts, axis=0) if len(parts) > 1 else parts[0])
    return multiply(left, op_hi, op_lo)


def product_half(code, parity, op_hi, op_lo):
    left = []
    for term in range(2):
        parts = []
        for o in range(5):
            pair = (parity + o) // 2
            at = pl.multiple_of((pair // 2) * 16, 16)
            parts.append(code[(parity + o) % 2, pair % 2, term, pl.ds(at, 128), :])
        left.append(jnp.concatenate(parts, axis=1))
    return multiply(left, op_hi, op_lo)


def far(d):
    return -(d[0] + (2 if d[1] == 2 else 1 if d[1] else 0))


AWAY = sorted([(dz, dy) for dz in range(4) for dy in range(4) if (dz, dy) != (0, 0)], key=far)
SENDS = ("ag1", "hand1", "qswap", "qsum", "qx", "swap1", "swap2", "rs1", "x", "ag2", "hand2", "xg", "swap3", "rs2")
SENDS += ("hop0", "hop1", "relay0", "relay1", "pass0", "pass1", "edge0", "edge1")
ARRIVALS = SENDS + ("ag1_1", "ag1_2", "ag1_3", "ag2_1", "ag2_2", "ag2_3")


def is_extra(u):
    return (u == 5) | (u == 6) | (u == 9) | (u == 10)


def extra_pair(u):
    return jnp.where(u < 8, u - 5, u + 9)


def kernel(
    exp_hbm, sky_ref, ker_ref, cov_ref, out_ref,
    exp_ref, kpad, rows, fwd_hi, fwd_lo, flip_hi, flip_lo, mid, near, rmid, rnear, hmid, hnear, code, rcode, hcode,
    own, prev, follow, model, exp_prev, exp_follow, expo, norms,
    q_all, q_core, q_sum, q_in, qx_in, nums, r_core, a_sum, r_in, x_in, nums2, r_core2, a_sum2, r_in2,
    exp_sem, send_sems, recv_sems,
):
    t = lax.axis_index("tile")
    v = lax.axis_index("visit")
    tiles = lax.axis_size("tile")
    z, y, c = v // 8, (v // 2) % 4, v % 2
    u = v // 2

    def chip(d):
        return ((z + d[0]) % 4) * 4 + (y + d[1]) % 4

    def there(d):
        return {"visit": 2 * chip(d) + c, "tile": t}

    partner = {"visit": 2 * u + (1 - c), "tile": t}
    up = {"visit": v, "tile": t + 1}
    down = {"visit": v, "tile": t - 1}
    has_up = t < tiles - 1
    has_down = t > 0
    extra = is_extra(u)

    prev[...] = jnp.zeros_like(prev)
    follow[...] = jnp.zeros_like(follow)
    barrier = pltpu.get_barrier_semaphore()
    for peer in [there(d) for d in AWAY] + [partner]:
        pl.semaphore_signal(barrier, inc=1, device_id=peer, device_id_type=MESH)

    @pl.when(has_up)
    def _():
        pl.semaphore_signal(barrier, inc=1, device_id=up, device_id_type=MESH)

    @pl.when(has_down)
    def _():
        pl.semaphore_signal(barrier, inc=1, device_id=down, device_id_type=MESH)

    load = pltpu.make_async_copy(exp_hbm.at[0], exp_ref, exp_sem)
    load.start()

    def remote(src, dst, name, device, arrival=None):
        return pltpu.make_async_remote_copy(
            src_ref=src,
            dst_ref=dst,
            send_sem=send_sems.at[SENDS.index(name)],
            recv_sem=recv_sems.at[ARRIVALS.index(arrival or name)],
            device_id=device,
            device_id_type=MESH,
        )

    def got(ref, name):
        remote(ref, ref, "ag1", partner, name).wait_recv()

    def gone(ref, name):
        remote(ref, ref, name, partner).wait_send()

    def when(cond, act):
        pl.when(cond)(act)

    own[c, u] = block_swap(sky_ref[...])
    kpad[...] = jnp.zeros_like(kpad)
    raw = ker_ref[:, 0, :]
    kpad[0:31, 0:31] = raw / jnp.sum(raw)
    w_here = cov_ref[0, t].astype(F32)
    w_down = jnp.where(has_down, cov_ref[0, jnp.maximum(t - 1, 0)], 0).astype(F32)
    w_up = jnp.where(has_up, cov_ref[0, jnp.minimum(t + 1, tiles - 1)], 0).astype(F32)
    i128, a32 = iota((128, 32), 0), iota((128, 32), 1)
    weights = jnp.where(
        i128 < 64,
        jnp.where(i128 + a32 < 47, w_down, w_here),
        jnp.where(i128 + a32 >= 111, w_up, w_here),
    )
    lines = jnp.dot(weights, kpad[...], precision=HI, preferred_element_type=F32)
    for b in range(40):
        at = 8 * b if b < 8 else 64 + 8 * (b - 32) if b >= 32 else 48
        q_all[b % 2, b // 2] = lines[at : at + 8]
    turn_rows = (iota((32, 32), 0) + iota((32, 32), 1) == 30).astype(F32)
    turn_cols = (iota((128, 128), 0) + iota((128, 128), 1) == 30).astype(F32)
    turned = jnp.dot(turn_rows, kpad[...], precision=HI, preferred_element_type=F32)
    turned = jnp.dot(turned, turn_cols, precision=HI, preferred_element_type=F32)
    build_rows(turned, rows)
    build_operator(rows, flip_hi, flip_lo)

    pl.semaphore_wait(barrier, 16 + has_up.astype(jnp.int32) + has_down.astype(jnp.int32))

    edge_up = remote(exp_ref.at[208:256, :], exp_prev, "edge0", up)
    edge_down = remote(exp_ref.at[0:48, :], exp_follow, "edge1", down)
    mine = own.at[c, u]
    hop_up = remote(mine, prev.at[c, u % 4], "hop0", up)
    hop_down = remote(mine, follow.at[c, u % 4], "hop1", down)
    last = u >= 12
    first = u < 4

    def relay_up():
        got(prev.at[c, u % 4], "hop0")
        block = prev.at[c, u % 4]
        for d in AWAY:
            remote(block, block, "relay0", there(d)).start()

    def relay_down():
        got(follow.at[c, u % 4], "hop1")
        block = follow.at[c, u % 4]
        for d in AWAY:
            remote(block, block, "relay1", there(d)).start()

    def hand_over(halo, name, relayed, comes, relayer):
        when(comes & relayer, lambda: got(halo.at[c, 0:3], relayed))
        when(comes & jnp.logical_not(relayer), lambda: got(halo.at[c], relayed))
        when(comes, lambda: remote(halo.at[c], halo.at[c], name, partner).start())

    when(last & has_up, hop_up.start)
    when(first & has_down, hop_down.start)
    for d in AWAY:
        remote(mine, mine, "ag1", there(d), ("ag1", "ag1_1", "ag1_2", "ag1_3")[d[0]]).start()
    remote(q_all.at[1 - c], q_core, "qswap", partner).start()
    load.wait()
    when(has_up, edge_up.start)
    when(has_down, edge_down.start)
    build_rows(kpad[...], rows)
    build_operator(rows, fwd_hi, fwd_lo)
    when(last & has_down, relay_up)
    when(first & has_up, relay_down)

    def swap_exposure(i, carry):
        for j in range(4):
            at = pl.multiple_of(32 * i + 8 * j, 8)
            expo[4 * i + j + 6] = block_swap(exp_ref[pl.ds(at, 8), :])
        return carry

    lax.fori_loop(0, 8, swap_exposure, 0)

    for dz, name in enumerate(("ag1", "ag1_1", "ag1_2", "ag1_3")):
        got(own.at[c, 0 : 4 if dz else 3], name)
        part = own.at[c, pl.ds(((z - dz) % 4) * 4, 4)]
        remote(part, part, "hand1", partner).start()
    got(q_core, "qswap")
    q_sum[...] = q_all[c] + q_core[...]
    for i, d in enumerate(AWAY):
        remote(q_sum.at[chip(d) + 2], q_in.at[i], "qsum", there(d)).start()
    for i, d in enumerate(AWAY):
        when(is_extra(chip(d)), remote(q_sum.at[extra_pair(chip(d))], qx_in.at[i], "qx", there(d)).start)
    got(own.at[c], "hand1")

    for g in range(4):
        put(weave(own, 4 * g, 4), 64 + 64 * g, mid, near)
    encode_rows(mid, near, code, 0, 64, 320)
    encode_rows(mid, near, code, 1, 64, 304)
    blurred = product(code, ((8, 28),), flip_hi, flip_lo)
    value = w_here * expo[8:36].reshape(224, 256) / blurred
    for g in range(7):
        put(value[32 * g : 32 * g + 32], 64 + 32 * g, rmid, rnear)
    encode_rows(rmid, rnear, rcode, 0, 64, 288)
    encode_rows(rmid, rnear, rcode, 1, 64, 272)

    far_prev = t == tiles // 2
    far_follow = t == tiles // 2 - 1
    hand_over(prev, "pass0", "relay0", has_down & jnp.logical_not(far_prev), last)
    hand_over(follow, "pass1", "relay1", has_up & jnp.logical_not(far_follow), first)
    found = product(rcode, ((8, 24),), fwd_hi, fwd_lo).reshape(12, 2, 8, 256)
    for k in range(2):
        nums[k, 4:16] = found[:, k]
    remote(nums.at[1 - c, 4:16], r_core.at[4:16], "swap1", partner).start()
    hand_over(prev, "pass0", "relay0", far_prev, last)
    hand_over(follow, "pass1", "relay1", far_follow, first)

    when(has_down, lambda: got(exp_prev, "edge0"))
    when(has_up, lambda: got(exp_follow, "edge1"))

    def swap_edges(i, carry):
        at = pl.multiple_of(8 * i, 8)
        expo[i] = block_swap(exp_prev[pl.ds(at, 8), :])
        expo[38 + i] = block_swap(exp_follow[pl.ds(at, 8), :])
        return carry

    lax.fori_loop(0, 6, swap_edges, 0, unroll=2)
    got(r_core.at[4:16], "swap1")
    a_sum[4:16] = nums[c, 4:16] + r_core[4:16]

    def at_edge(place):
        return (place < 2) | (place >= 14)

    spread = [remote(a_sum.at[chip(d) + 2], r_in.at[i], "rs1", there(d)) for i, d in enumerate(AWAY)]
    x_spread = [remote(a_sum.at[extra_pair(chip(d))], x_in.at[i], "x", there(d)) for i, d in enumerate(AWAY)]
    for d, copy in zip(AWAY, spread):
        when(jnp.logical_not(at_edge(chip(d))), copy.start)

    when(has_down, lambda: got(prev.at[1 - c], "pass0"))
    when(has_up, lambda: got(follow.at[1 - c], "pass1"))
    put(weave(prev, 0, 4), 0, mid, near)
    put(weave(follow, 0, 4), 320, mid, near)
    encode_rows(mid, near, code, 0, 0, 64)
    encode_rows(mid, near, code, 1, 0, 64)
    encode_rows(mid, near, code, 0, 320, 384)
    encode_rows(mid, near, code, 1, 304, 368)
    blurred = product(code, ((0, 8), (36, 8)), flip_hi, flip_lo)
    for low, source, count, weight, comes in (
        (0, 0, 6, w_down, has_down),
        (6, 48, 2, w_here, None),
        (36, 64, 2, w_here, None),
        (38, 80, 6, w_up, has_up),
    ):
        m = 8 * count
        value = weight * expo[low : low + count].reshape(m, 256) / blurred[source : source + m]
        if comes is not None:
            value = jnp.where(comes, value, 0.0)
        put(value, 8 * low, rmid, rnear)
    encode_rows(rmid, rnear, rcode, 0, 0, 64)
    encode_rows(rmid, rnear, rcode, 1, 0, 64)
    encode_rows(rmid, rnear, rcode, 0, 288, 352)
    encode_rows(rmid, rnear, rcode, 1, 272, 336)
    found = product(rcode, ((0, 8), (32, 8)), fwd_hi, fwd_lo).reshape(8, 2, 8, 256)
    for k in range(2):
        nums[k, 0:4] = found[0:4, k]
        nums[k, 16:20] = found[4:8, k]
    for at in (0, 16):
        remote(nums.at[1 - c, at : at + 4], r_core.at[at : at + 4], "swap2", partner).start()

    def normal(line):
        cover = iota((128, 256), 1) + iota((128, 256), 0) - 15
        valid = ((cover >= 0) & (cover < 256) & (iota((128, 256), 0) < 31)).astype(F32)
        return block_swap(jnp.dot(line, valid, precision=HI, preferred_element_type=F32))

    def total_of(own_part, parts):
        total = own_part
        for i in range(15):
            total = total + parts[i]
        return total

    got(q_in, "qsum")
    norm = normal(total_of(q_sum[u + 2], q_in))
    pair = jnp.where(extra, extra_pair(u), 0)

    @pl.when(extra)
    def _():
        got(qx_in, "qx")
        norms[...] = normal(total_of(q_sum[pair], qx_in))

    got(r_core.at[0:8], "swap2")
    for at in (0, 16):
        a_sum[at : at + 4] = nums[c, at : at + 4] + r_core[at : at + 4]
    for d, copy, x_copy in zip(AWAY, spread, x_spread):
        when(at_edge(chip(d)), copy.start)
        when(is_extra(chip(d)), x_copy.start)

    got(r_in, "rs1")
    model[c, u + 2] = own[c, u] * total_of(a_sum[u + 2], r_in) / norm

    mine = model.at[c, u + 2]
    for d in AWAY:
        remote(mine, mine, "ag2", there(d), ("ag2", "ag2_1", "ag2_2", "ag2_3")[d[0]]).start()

    @pl.when(extra)
    def _():
        got(x_in, "x")
        before = prev[c, jnp.where(u < 8, u - 3, 2)]
        after = follow[c, jnp.where(u < 8, 0, u - 9)]
        exists = jnp.where(u < 8, has_down.astype(jnp.int32), has_up.astype(jnp.int32)) > 0
        old = jnp.where(u < 8, before, after)
        new = old * total_of(a_sum[pair], x_in) / norms[...]
        model[c, pair] = jnp.where(exists, new, 0.0)
        block = model.at[c, pair]
        for d in AWAY:
            remote(block, block, "xg", there(d)).start()

    for dz, name in enumerate(("ag2", "ag2_1", "ag2_2", "ag2_3")):
        got(model.at[c, 0 : 4 if dz else 3], name)
        part = model.at[c, pl.ds(((z - dz) % 4) * 4 + 2, 4)]
        remote(part, part, "hand2", partner).start()
    when(extra, lambda: got(model.at[c, 0:3], "xg"))
    when(jnp.logical_not(extra), lambda: got(model.at[c, 0:4], "xg"))
    for at in (0, 18):
        part = model.at[c, at : at + 2]
        remote(part, part, "hand2", partner).start()
    got(model.at[c], "hand2")

    for g in range(5):
        put(weave(model, 4 * g, 4), 64 * g, mid, near)
    encode_rows(mid, near, code, 0, 0, 320)
    encode_rows(mid, near, code, 1, 0, 304)
    blurred = product(code, ((0, 36),), flip_hi, flip_lo)
    for low, count, weight, comes in ((0, 2, w_down, has_down), (2, 32, w_here, None), (34, 2, w_up, has_up)):
        for g in range(low, low + count, 4):
            n = min(4, low + count - g)
            value = weight * expo[g + 4 : g + 4 + n].reshape(8 * n, 256) / blurred[8 * g : 8 * g + 8 * n]
            if comes is not None:
                value = jnp.where(comes, value, 0.0)
            hmid[g // 2 : (g + n) // 2] = value.reshape(n // 2, 2, 8, 256)
            hnear[g // 2 : (g + n) // 2] = beside(value).reshape(n // 2, 2, 8, 256)
    for parity in range(2):
        for shift, count in ((0, 18), (1, 16)):
            for k, src in ((0, hmid), (1, hnear)):
                value = src[shift : shift + count, parity].reshape(8 * count, 256)
                lanes = slice(256 * k, 256 * k + 256)
                encode(value, hcode.at[parity, shift], slice(0, 8 * count), lanes)
    nums2[0] = product_half(hcode, 1 - c, fwd_hi, fwd_lo).reshape(16, 8, 256)
    remote(nums2.at[0], r_core2, "swap3", partner).start()
    nums2[1] = product_half(hcode, c, fwd_hi, fwd_lo).reshape(16, 8, 256)
    got(r_core2, "swap3")
    a_sum2[...] = nums2[1] + r_core2[...]
    for i, d in enumerate(AWAY):
        remote(a_sum2.at[chip(d)], r_in2.at[i], "rs2", there(d)).start()
    got(r_in2, "rs2")
    out_ref[...] = block_swap(model[c, u + 2] * total_of(a_sum2[u], r_in2) / norm)

    for name in ("ag1", "rs1", "ag2", "rs2"):
        gone(r_in, name)
    gone(own.at[c], "hand1")
    gone(q_core, "qswap")
    gone(q_in, "qsum")
    gone(r_core.at[4:16], "swap1")
    gone(r_core.at[0:8], "swap2")
    gone(model.at[c], "hand2")
    gone(r_core2, "swap3")
    for ref, name in ((q_in, "qx"), (x_in, "x")):
        when(extra, lambda ref=ref, name=name: gone(ref.at[0:3], name))
        when(jnp.logical_not(extra), lambda ref=ref, name=name: gone(ref.at[0:4], name))
    when(extra, lambda: gone(x_in, "xg"))
    when(has_up, lambda: gone(exp_prev, "edge0"))
    when(has_down, lambda: gone(exp_follow, "edge1"))
    when(last & has_up, lambda: gone(prev.at[c, 0], "hop0"))
    when(first & has_down, lambda: gone(prev.at[c, 0], "hop1"))
    when(last & has_down, lambda: gone(x_in, "relay0"))
    when(first & has_up, lambda: gone(x_in, "relay1"))
    when(has_down, lambda: gone(prev.at[c], "pass0"))
    when(has_up, lambda: gone(prev.at[c], "pass1"))


def body(exposures, sky_model, blur_kernels, coverage):
    vmem = pl.BlockSpec(memory_space=pltpu.VMEM)
    V = pltpu.VMEM
    D = pltpu.SemaphoreType.DMA
    op = V((7, 2, 8, 32, 256), BF)

    def blocks(*dims):
        return V((*dims, 8, 256), F32)

    def lanes(*dims):
        return V((*dims, 8, 128), F32)

    return pl.pallas_call(
        kernel,
        out_shape=jax.ShapeDtypeStruct((8, 256), F32),
        in_specs=[pl.BlockSpec(memory_space=pl.ANY), vmem, vmem, pl.BlockSpec(memory_space=pltpu.SMEM)],
        out_specs=vmem,
        scratch_shapes=[
            V((256, 256), F32), V((32, 128), F32), V((48, 128), F32), op, op, op, op,
            V((384, 256), F32), V((384, 256), F32), V((352, 256), F32), V((352, 256), F32),
            blocks(18, 2), blocks(18, 2), V((2, 2, 384, 512), BF), V((2, 2, 352, 512), BF), V((2, 2, 2, 144, 512), BF),
            blocks(2, 16), blocks(2, 4), blocks(2, 4), blocks(2, 20), V((48, 256), F32), V((48, 256), F32), blocks(44),
            V((8, 256), F32),
            lanes(2, 20), lanes(20), lanes(20), lanes(15), lanes(15),
            blocks(2, 20), blocks(20), blocks(20), blocks(15), blocks(15), blocks(2, 16), blocks(16), blocks(16), blocks(15),
            D, D((len(SENDS),)), D((len(ARRIVALS),)),
        ],
        compiler_params=pltpu.CompilerParams(collective_id=0, has_side_effects=True),
    )(exposures, sky_model, jnp.transpose(blur_kernels, (1, 0, 2)), coverage)


def solution(mesh):
    return jax.shard_map(
        body,
        mesh=mesh,
        in_specs=(
            P("visit", "tile", None),
            P(("tile", "visit"), None),
            P("visit", None, None),
            P("visit", None),
        ),
        out_specs=P(("tile", "visit"), None),
        check_vma=False,
    )
```

time: 644 us -> 49.7 us (0.08)
  waiting for transfers between devices: 424 us -> 0 us
  blocking collectives: 83.8 us -> 0 us
  matrix products: 59.2 us -> 0 us
  Pallas kernels: 0 us -> 48.2 us
  starting transfers between devices: 32.8 us -> 0 us
  local copies, waits for them, and re-layouts: 20.3 us -> 1.3 us
  between operations: 13.3 us -> 0.01 us
  other arithmetic: 9.28 us -> 0 us
    reduce_scatter x3 -> x0, waiting for transfers between devices: 407 us -> none  [the longest x2 285 us: body(): lax.psum_scatter(numerator, 'visit', scatter_dimension=0, tiled=True)]
    all_gather x2 -> x0, blocking collectives: 83.8 us -> none  [body(): whole = lax.all_gather(model_shard, 'visit', axis=0, tiled=True)]
    dot_general x8 -> x0, matrix products: 59.2 us -> none  [the longest x4 44.8 us: correlate(): product = jnp.dot(extended, operator, precision=lax.Precision.HIGHEST)]
    pallas_call x0 -> x1, Pallas kernels: none -> 48.2 us  [body(): pl.pallas_call(kernel, out_shape=jax.ShapeDtypeStruct((8, 256), F32), in_...]
    ppermute x8 -> x0, starting transfers between devices: 32.6 us -> none  [the longest x4 22.7 us: padded(): before = lax.ppermute(last, axis, up)]
    transpose x2 -> x0, local copies, waits for them, and re-layouts: 19.9 us -> none  [column_operator(): operator = operator.reshape(width, width, kernel_len).transpose(0, 2, 1)]
    ppermute x8 -> x0, waiting for transfers between devices: 17.2 us -> none  [the longest x4 17.2 us: padded(): after = lax.ppermute(initial, axis, down)]
  transfers between devices with their start and end apart: 11 -> 0, of which waited for: 5 -> 0; matrix products, arithmetic and copies ran while one was open for 8% -> 0% of each run, Pallas kernels for 0% -> 0%
where the time goes in v3:
time: 49.7 us; the launch traced here: 49.5 us
  Pallas kernels  48.2 us (97%)
  local copies, waits for them, and re-layouts  1.3 us (3%)
    pallas_call x1, Pallas kernels, body(): pl.pallas_call(kernel, out_shape=jax.ShapeDtypeStruct((8, 256), F32), in_...  48.2 us
    unnamed x1, local copies, waits for them, and re-layouts  1.3 us

profile of v3, /device:TPU:6, one launch (start us, length us, event | category | flops | bytes accessed | tf_op | source)
XLA Modules:
  0.0 49.5 jit_solution(4925612699419069570)
XLA Ops:
  0.0 48.2 %shard_map.46 = f32[8,256]{1,0:T(8,128)} custom-call(f32[1,256,256]{2,1,0:T(8,128)} %exp_hbm.1, f32[8,256]{1,0:T(8,128)} %sky_ref.1, f32[31,1,31]{2,1,0:T(1,128)} %bitcast.1, s32[1,8]{1,0:T(1,128)} %cov_ref.1), custom_call_target="tpu_custom_call" | custom-call | tf_op jit(solution)/shard_map/pallas_call | solution.py:488
  48.2 1.3 %copy.6 = f32[8,256]{1,0:T(8,128)} copy(f32[8,256]{1,0:T(8,128)} %shard_map.46) | data formatting | bytes 16384

commit v4 on v3

--- a/solution.py
+++ b/solution.py
@@ -132,7 +132,7 @@
 AWAY = sorted([(dz, dy) for dz in range(4) for dy in range(4) if (dz, dy) != (0, 0)], key=far)
 SENDS = ("ag1", "hand1", "qswap", "qsum", "qx", "swap1", "swap2", "rs1", "x", "ag2", "hand2", "xg", "swap3", "rs2")
 SENDS += ("hop0", "hop1", "relay0", "relay1", "pass0", "pass1", "edge0", "edge1")
-ARRIVALS = SENDS + ("ag1_1", "ag1_2", "ag1_3", "ag2_1", "ag2_2", "ag2_3")
+ARRIVALS = ("ag1_0", "ag1_1", "ag1_2", "ag1_3", "ag2_0", "ag2_1", "ag2_2", "ag2_3") + SENDS
 
 
 def is_extra(u):
@@ -144,11 +144,11 @@
 
 
 def kernel(
-    exp_hbm, sky_ref, ker_ref, cov_ref, out_ref,
-    exp_ref, kpad, rows, fwd_hi, fwd_lo, flip_hi, flip_lo, mid, near, rmid, rnear, hmid, hnear, code, rcode, hcode,
+    exp_hbm, sky_hbm, ker_hbm, cov_hbm, out_ref,
+    exp_ref, sky_ref, ker_ref, cov_ref, kpad, rows, fwd_hi, fwd_lo, flip_hi, flip_lo, mid, near, rmid, rnear, hmid, hnear, code, rcode, hcode,
     own, prev, follow, model, exp_prev, exp_follow, expo, norms,
     q_all, q_core, q_sum, q_in, qx_in, nums, r_core, a_sum, r_in, x_in, nums2, r_core2, a_sum2, r_in2,
-    exp_sem, send_sems, recv_sems,
+    load_sems, send_sems, recv_sems,
 ):
     t = lax.axis_index("tile")
     v = lax.axis_index("visit")
@@ -169,6 +169,14 @@
     has_down = t > 0
     extra = is_extra(u)
 
+    loads = [
+        pltpu.make_async_copy(src, dst, load_sems.at[i])
+        for i, (src, dst) in enumerate(
+            ((ker_hbm, ker_ref), (cov_hbm, cov_ref), (sky_hbm, sky_ref), (exp_hbm.at[0], exp_ref))
+        )
+    ]
+    for copy in loads:
+        copy.start()
     prev[...] = jnp.zeros_like(prev)
     follow[...] = jnp.zeros_like(follow)
     barrier = pltpu.get_barrier_semaphore()
@@ -183,21 +191,18 @@
     def _():
         pl.semaphore_signal(barrier, inc=1, device_id=down, device_id_type=MESH)
 
-    load = pltpu.make_async_copy(exp_hbm.at[0], exp_ref, exp_sem)
-    load.start()
-
     def remote(src, dst, name, device, arrival=None):
         return pltpu.make_async_remote_copy(
             src_ref=src,
             dst_ref=dst,
             send_sem=send_sems.at[SENDS.index(name)],
-            recv_sem=recv_sems.at[ARRIVALS.index(arrival or name)],
+            recv_sem=recv_sems.at[ARRIVALS.index(name) if arrival is None else arrival],
             device_id=device,
             device_id_type=MESH,
         )
 
     def got(ref, name):
-        remote(ref, ref, "ag1", partner, name).wait_recv()
+        remote(ref, ref, "ag1", partner, ARRIVALS.index(name)).wait_recv()
 
     def gone(ref, name):
         remote(ref, ref, name, partner).wait_send()
@@ -205,10 +210,11 @@
     def when(cond, act):
         pl.when(cond)(act)
 
-    own[c, u] = block_swap(sky_ref[...])
     kpad[...] = jnp.zeros_like(kpad)
+    loads[0].wait()
     raw = ker_ref[:, 0, :]
     kpad[0:31, 0:31] = raw / jnp.sum(raw)
+    loads[1].wait()
     w_here = cov_ref[0, t].astype(F32)
     w_down = jnp.where(has_down, cov_ref[0, jnp.maximum(t - 1, 0)], 0).astype(F32)
     w_up = jnp.where(has_up, cov_ref[0, jnp.minimum(t + 1, tiles - 1)], 0).astype(F32)
@@ -222,6 +228,8 @@
     for b in range(40):
         at = 8 * b if b < 8 else 64 + 8 * (b - 32) if b >= 32 else 48
         q_all[b % 2, b // 2] = lines[at : at + 8]
+    loads[2].wait()
+    own[c, u] = block_swap(sky_ref[...])
     turn_rows = (iota((32, 32), 0) + iota((32, 32), 1) == 30).astype(F32)
     turn_cols = (iota((128, 128), 0) + iota((128, 128), 1) == 30).astype(F32)
     turned = jnp.dot(turn_rows, kpad[...], precision=HI, preferred_element_type=F32)
@@ -259,9 +267,9 @@
     when(last & has_up, hop_up.start)
     when(first & has_down, hop_down.start)
     for d in AWAY:
-        remote(mine, mine, "ag1", there(d), ("ag1", "ag1_1", "ag1_2", "ag1_3")[d[0]]).start()
+        remote(mine, mine, "ag1", there(d), z).start()
     remote(q_all.at[1 - c], q_core, "qswap", partner).start()
-    load.wait()
+    loads[3].wait()
     when(has_up, edge_up.start)
     when(has_down, edge_down.start)
     build_rows(kpad[...], rows)
@@ -277,9 +285,13 @@
 
     lax.fori_loop(0, 8, swap_exposure, 0)
 
-    for dz, name in enumerate(("ag1", "ag1_1", "ag1_2", "ag1_3")):
-        got(own.at[c, 0 : 4 if dz else 3], name)
-        part = own.at[c, pl.ds(((z - dz) % 4) * 4, 4)]
+    def got_row(ref, row, name):
+        when(z == row, lambda: got(ref.at[c, 0:3], name))
+        when(z != row, lambda: got(ref.at[c, 0:4], name))
+
+    for row in (1, 2, 0, 3):
+        got_row(own, row, "ag1_%d" % row)
+        part = own.at[c, 4 * row : 4 * row + 4]
         remote(part, part, "hand1", partner).start()
     got(q_core, "qswap")
     q_sum[...] = q_all[c] + q_core[...]
@@ -395,7 +407,7 @@
 
     mine = model.at[c, u + 2]
     for d in AWAY:
-        remote(mine, mine, "ag2", there(d), ("ag2", "ag2_1", "ag2_2", "ag2_3")[d[0]]).start()
+        remote(mine, mine, "ag2", there(d), 4 + z).start()
 
     @pl.when(extra)
     def _():
@@ -410,9 +422,9 @@
         for d in AWAY:
             remote(block, block, "xg", there(d)).start()
 
-    for dz, name in enumerate(("ag2", "ag2_1", "ag2_2", "ag2_3")):
-        got(model.at[c, 0 : 4 if dz else 3], name)
-        part = model.at[c, pl.ds(((z - dz) % 4) * 4 + 2, 4)]
+    for row in (1, 2, 0, 3):
+        got_row(model, row, "ag2_%d" % row)
+        part = model.at[c, 4 * row + 2 : 4 * row + 6]
         remote(part, part, "hand2", partner).start()
     when(extra, lambda: got(model.at[c, 0:3], "xg"))
     when(jnp.logical_not(extra), lambda: got(model.at[c, 0:4], "xg"))
@@ -488,17 +500,18 @@
     return pl.pallas_call(
         kernel,
         out_shape=jax.ShapeDtypeStruct((8, 256), F32),
-        in_specs=[pl.BlockSpec(memory_space=pl.ANY), vmem, vmem, pl.BlockSpec(memory_space=pltpu.SMEM)],
+        in_specs=[pl.BlockSpec(memory_space=pl.ANY)] * 4,
         out_specs=vmem,
         scratch_shapes=[
-            V((256, 256), F32), V((32, 128), F32), V((48, 128), F32), op, op, op, op,
+            V((256, 256), F32), V((8, 256), F32), V((31, 1, 31), F32), pltpu.SMEM((1, 8), jnp.int32),
+            V((32, 128), F32), V((48, 128), F32), op, op, op, op,
             V((384, 256), F32), V((384, 256), F32), V((352, 256), F32), V((352, 256), F32),
             blocks(18, 2), blocks(18, 2), V((2, 2, 384, 512), BF), V((2, 2, 352, 512), BF), V((2, 2, 2, 144, 512), BF),
             blocks(2, 16), blocks(2, 4), blocks(2, 4), blocks(2, 20), V((48, 256), F32), V((48, 256), F32), blocks(44),
             V((8, 256), F32),
             lanes(2, 20), lanes(20), lanes(20), lanes(15), lanes(15),
             blocks(2, 20), blocks(20), blocks(20), blocks(15), blocks(15), blocks(2, 16), blocks(16), blocks(16), blocks(15),
-            D, D((len(SENDS),)), D((len(ARRIVALS),)),
+            D((4,)), D((len(SENDS),)), D((len(ARRIVALS),)),
         ],
         compiler_params=pltpu.CompilerParams(collective_id=0, has_side_effects=True),
     )(exposures, sky_model, jnp.transpose(blur_kernels, (1, 0, 2)), coverage)

time: 49.7 us -> 48.7 us (0.980)
  Pallas kernels: 48.2 us -> 47.2 us
    pallas_call x1, Pallas kernels: 48.2 us -> 47.2 us  [body(): pl.pallas_call(kernel, out_shape=jax.ShapeDtypeStruct((8, 256), F32), in_...]
where the time goes in v4:
time: 48.7 us; the launch traced here: 48.5 us
  Pallas kernels  47.2 us (97%)
  local copies, waits for them, and re-layouts  1.3 us (3%)
    pallas_call x1, Pallas kernels, body(): pl.pallas_call(kernel, out_shape=jax.ShapeDtypeStruct((8, 256), F32), in_...  47.2 us
    unnamed x1, local copies, waits for them, and re-layouts  1.3 us

profile of v4, /device:TPU:6, one launch (start us, length us, event | category | flops | bytes accessed | tf_op | source)
XLA Modules:
  0.0 48.5 jit_solution(13003677939931239731)
XLA Ops:
  0.0 47.2 %shard_map.46 = f32[8,256]{1,0:T(8,128)} custom-call(f32[1,256,256]{2,1,0:T(8,128)} %exp_hbm.1, f32[8,256]{1,0:T(8,128)} %sky_hbm.1, f32[31,1,31]{2,1,0:T(1,128)} %bitcast.1, s32[1,8]{1,0:T(1,128)} %cov_hbm.1), custom_call_target="tpu_custom_call" | custom-call | tf_op jit(solution)/shard_map/pallas_call | solution.py:500
  47.2 1.3 %copy.6 = f32[8,256]{1,0:T(8,128)} copy(f32[8,256]{1,0:T(8,128)} %shard_map.46) | data formatting | bytes 16384

commit v5 on v4

--- a/solution.py
+++ b/solution.py
@@ -113,26 +113,14 @@
     return multiply(left, op_hi, op_lo)
 
 
-def product_half(code, parity, op_hi, op_lo):
-    left = []
-    for term in range(2):
-        parts = []
-        for o in range(5):
-            pair = (parity + o) // 2
-            at = pl.multiple_of((pair // 2) * 16, 16)
-            parts.append(code[(parity + o) % 2, pair % 2, term, pl.ds(at, 128), :])
-        left.append(jnp.concatenate(parts, axis=1))
-    return multiply(left, op_hi, op_lo)
-
-
 def far(d):
     return -(d[0] + (2 if d[1] == 2 else 1 if d[1] else 0))
 
 
 AWAY = sorted([(dz, dy) for dz in range(4) for dy in range(4) if (dz, dy) != (0, 0)], key=far)
 SENDS = ("ag1", "hand1", "qswap", "qsum", "qx", "swap1", "swap2", "rs1", "x", "ag2", "hand2", "xg", "swap3", "rs2")
-SENDS += ("hop0", "hop1", "relay0", "relay1", "pass0", "pass1", "edge0", "edge1")
-ARRIVALS = ("ag1_0", "ag1_1", "ag1_2", "ag1_3", "ag2_0", "ag2_1", "ag2_2", "ag2_3") + SENDS
+SENDS += ("ag2o", "xgo", "swap4", "hop0", "hop1", "relay0", "relay1", "pass0", "pass1", "edge0", "edge1")
+ARRIVALS = ("ag1_0", "ag1_1", "ag1_2", "ag1_3", "ag2_0", "ag2_1", "ag2_2", "ag2_3", "ag2_late") + SENDS
 
 
 def is_extra(u):
@@ -145,7 +133,7 @@
 
 def kernel(
     exp_hbm, sky_hbm, ker_hbm, cov_hbm, out_ref,
-    exp_ref, sky_ref, ker_ref, cov_ref, kpad, rows, fwd_hi, fwd_lo, flip_hi, flip_lo, mid, near, rmid, rnear, hmid, hnear, code, rcode, hcode,
+    exp_ref, sky_ref, ker_ref, cov_ref, kpad, rows, fwd_hi, fwd_lo, flip_hi, flip_lo, mid, near, rmid, rnear, code, rcode,
     own, prev, follow, model, exp_prev, exp_follow, expo, norms,
     q_all, q_core, q_sum, q_in, qx_in, nums, r_core, a_sum, r_in, x_in, nums2, r_core2, a_sum2, r_in2,
     load_sems, send_sems, recv_sems,
@@ -162,12 +150,20 @@
     def there(d):
         return {"visit": 2 * chip(d) + c, "tile": t}
 
+    def across(d):
+        return {"visit": 2 * chip(d) + 1 - c, "tile": t}
+
     partner = {"visit": 2 * u + (1 - c), "tile": t}
     up = {"visit": v, "tile": t + 1}
     down = {"visit": v, "tile": t - 1}
     has_up = t < tiles - 1
     has_down = t > 0
     extra = is_extra(u)
+
+    def at_edge(place):
+        return (place < 2) | (place >= 14)
+
+    late = at_edge(u)
 
     loads = [
         pltpu.make_async_copy(src, dst, load_sems.at[i])
@@ -293,12 +289,6 @@
         got_row(own, row, "ag1_%d" % row)
         part = own.at[c, 4 * row : 4 * row + 4]
         remote(part, part, "hand1", partner).start()
-    got(q_core, "qswap")
-    q_sum[...] = q_all[c] + q_core[...]
-    for i, d in enumerate(AWAY):
-        remote(q_sum.at[chip(d) + 2], q_in.at[i], "qsum", there(d)).start()
-    for i, d in enumerate(AWAY):
-        when(is_extra(chip(d)), remote(q_sum.at[extra_pair(chip(d))], qx_in.at[i], "qx", there(d)).start)
     got(own.at[c], "hand1")
 
     for g in range(4):
@@ -312,6 +302,13 @@
     encode_rows(rmid, rnear, rcode, 0, 64, 288)
     encode_rows(rmid, rnear, rcode, 1, 64, 272)
 
+    got(q_core, "qswap")
+    q_sum[...] = q_all[c] + q_core[...]
+    for i, d in enumerate(AWAY):
+        remote(q_sum.at[chip(d) + 2], q_in.at[i], "qsum", there(d)).start()
+    for i, d in enumerate(AWAY):
+        when(is_extra(chip(d)), remote(q_sum.at[extra_pair(chip(d))], qx_in.at[i], "qx", there(d)).start)
+
     far_prev = t == tiles // 2
     far_follow = t == tiles // 2 - 1
     hand_over(prev, "pass0", "relay0", has_down & jnp.logical_not(far_prev), last)
@@ -335,9 +332,6 @@
     lax.fori_loop(0, 6, swap_edges, 0, unroll=2)
     got(r_core.at[4:16], "swap1")
     a_sum[4:16] = nums[c, 4:16] + r_core[4:16]
-
-    def at_edge(place):
-        return (place < 2) | (place >= 14)
 
     spread = [remote(a_sum.at[chip(d) + 2], r_in.at[i], "rs1", there(d)) for i, d in enumerate(AWAY)]
     x_spread = [remote(a_sum.at[extra_pair(chip(d))], x_in.at[i], "x", there(d)) for i, d in enumerate(AWAY)]
@@ -406,8 +400,14 @@
     model[c, u + 2] = own[c, u] * total_of(a_sum[u + 2], r_in) / norm
 
     mine = model.at[c, u + 2]
+    arrival = jnp.where(late, ARRIVALS.index("ag2_late"), ARRIVALS.index("ag2_0") + z)
     for d in AWAY:
-        remote(mine, mine, "ag2", there(d), 4 + z).start()
+        remote(mine, mine, "ag2", there(d), arrival).start()
+
+    @pl.when(late)
+    def _():
+        for d in AWAY + [(0, 0)]:
+            remote(mine, mine, "ag2o", across(d)).start()
 
     @pl.when(extra)
     def _():
@@ -421,44 +421,79 @@
         block = model.at[c, pair]
         for d in AWAY:
             remote(block, block, "xg", there(d)).start()
-
-    for row in (1, 2, 0, 3):
-        got_row(model, row, "ag2_%d" % row)
-        part = model.at[c, 4 * row + 2 : 4 * row + 6]
+        for d in AWAY + [(0, 0)]:
+            remote(block, block, "xgo", across(d)).start()
+
+    def got_all(ref, count, mine_too, name):
+        when(mine_too, lambda: got(ref.at[c, 0 : count - 1], name))
+        when(jnp.logical_not(mine_too), lambda: got(ref.at[c, 0:count], name))
+
+    for row, low, high in ((1, 6, 10), (2, 10, 14), (0, 4, 6), (3, 14, 16)):
+        got_all(model, high - low, (z == row) & jnp.logical_not(late), "ag2_%d" % row)
+        part = model.at[c, low:high]
         remote(part, part, "hand2", partner).start()
-    when(extra, lambda: got(model.at[c, 0:3], "xg"))
-    when(jnp.logical_not(extra), lambda: got(model.at[c, 0:4], "xg"))
-    for at in (0, 18):
-        part = model.at[c, at : at + 2]
-        remote(part, part, "hand2", partner).start()
-    got(model.at[c], "hand2")
-
+    got(model.at[c, 0:12], "hand2")
+    for g in range(3):
+        put(weave(model, 4 + 4 * g, 4), 64 + 64 * g, mid, near)
+    encode_rows(mid, near, code, 0, 64, 256)
+    encode_rows(mid, near, code, 1, 64, 240)
+    blurred = product(code, ((8, 20),), flip_hi, flip_lo)
+    value = w_here * expo[12:32].reshape(160, 256) / blurred
     for g in range(5):
-        put(weave(model, 4 * g, 4), 64 * g, mid, near)
-    encode_rows(mid, near, code, 0, 0, 320)
-    encode_rows(mid, near, code, 1, 0, 304)
-    blurred = product(code, ((0, 36),), flip_hi, flip_lo)
-    for low, count, weight, comes in ((0, 2, w_down, has_down), (2, 32, w_here, None), (34, 2, w_up, has_up)):
-        for g in range(low, low + count, 4):
-            n = min(4, low + count - g)
-            value = weight * expo[g + 4 : g + 4 + n].reshape(8 * n, 256) / blurred[8 * g : 8 * g + 8 * n]
-            if comes is not None:
-                value = jnp.where(comes, value, 0.0)
-            hmid[g // 2 : (g + n) // 2] = value.reshape(n // 2, 2, 8, 256)
-            hnear[g // 2 : (g + n) // 2] = beside(value).reshape(n // 2, 2, 8, 256)
-    for parity in range(2):
-        for shift, count in ((0, 18), (1, 16)):
-            for k, src in ((0, hmid), (1, hnear)):
-                value = src[shift : shift + count, parity].reshape(8 * count, 256)
-                lanes = slice(256 * k, 256 * k + 256)
-                encode(value, hcode.at[parity, shift], slice(0, 8 * count), lanes)
-    nums2[0] = product_half(hcode, 1 - c, fwd_hi, fwd_lo).reshape(16, 8, 256)
-    remote(nums2.at[0], r_core2, "swap3", partner).start()
-    nums2[1] = product_half(hcode, c, fwd_hi, fwd_lo).reshape(16, 8, 256)
-    got(r_core2, "swap3")
-    a_sum2[...] = nums2[1] + r_core2[...]
-    for i, d in enumerate(AWAY):
-        remote(a_sum2.at[chip(d)], r_in2.at[i], "rs2", there(d)).start()
+        put(value[32 * g : 32 * g + 32], 64 + 32 * g, rmid, rnear)
+    encode_rows(rmid, rnear, rcode, 0, 64, 224)
+    encode_rows(rmid, rnear, rcode, 1, 64, 208)
+    found = product(rcode, ((8, 16),), fwd_hi, fwd_lo).reshape(8, 2, 8, 256)
+    for k in range(2):
+        nums2[k, 4:12] = found[:, k]
+    remote(nums2.at[1 - c, 4:12], r_core2.at[4:12], "swap3", partner).start()
+    got(r_core2.at[4:12], "swap3")
+    a_sum2[4:12] = nums2[c, 4:12] + r_core2[4:12]
+    spread = [remote(a_sum2.at[chip(d)], r_in2.at[i], "rs2", there(d)) for i, d in enumerate(AWAY)]
+
+    def inner(place):
+        return (place >= 4) & (place < 12)
+
+    for d, copy in zip(AWAY, spread):
+        when(inner(chip(d)), copy.start)
+
+    got_all(model, 4, late, "ag2_late")
+    got_all(model, 4, extra, "xg")
+    got(model.at[c, 0:4], "ag2o")
+    got(model.at[c, 0:4], "xgo")
+    put(weave(model, 0, 4), 0, mid, near)
+    put(weave(model, 16, 4), 256, mid, near)
+    encode_rows(mid, near, code, 0, 0, 64)
+    encode_rows(mid, near, code, 1, 0, 64)
+    encode_rows(mid, near, code, 0, 256, 320)
+    encode_rows(mid, near, code, 1, 240, 304)
+    blurred = product(code, ((0, 8), (28, 8)), flip_hi, flip_lo)
+    for low, source, count, weight, comes in (
+        (0, 0, 2, w_down, has_down),
+        (2, 16, 6, w_here, None),
+        (28, 64, 6, w_here, None),
+        (34, 112, 2, w_up, has_up),
+    ):
+        m = 8 * count
+        value = weight * expo[low + 4 : low + 4 + count].reshape(m, 256) / blurred[source : source + m]
+        if comes is not None:
+            value = jnp.where(comes, value, 0.0)
+        put(value, 8 * low, rmid, rnear)
+    encode_rows(rmid, rnear, rcode, 0, 0, 64)
+    encode_rows(rmid, rnear, rcode, 1, 0, 64)
+    encode_rows(rmid, rnear, rcode, 0, 224, 288)
+    encode_rows(rmid, rnear, rcode, 1, 208, 272)
+    found = product(rcode, ((0, 8), (24, 8)), fwd_hi, fwd_lo).reshape(8, 2, 8, 256)
+    for k in range(2):
+        nums2[k, 0:4] = found[0:4, k]
+        nums2[k, 12:16] = found[4:8, k]
+    for at in (0, 12):
+        remote(nums2.at[1 - c, at : at + 4], r_core2.at[at : at + 4], "swap4", partner).start()
+    got(r_core2.at[0:8], "swap4")
+    for at in (0, 12):
+        a_sum2[at : at + 4] = nums2[c, at : at + 4] + r_core2[at : at + 4]
+    for d, copy in zip(AWAY, spread):
+        when(jnp.logical_not(inner(chip(d))), copy.start)
     got(r_in2, "rs2")
     out_ref[...] = block_swap(model[c, u + 2] * total_of(a_sum2[u], r_in2) / norm)
 
@@ -469,8 +504,11 @@
     gone(q_in, "qsum")
     gone(r_core.at[4:16], "swap1")
     gone(r_core.at[0:8], "swap2")
-    gone(model.at[c], "hand2")
-    gone(r_core2, "swap3")
+    gone(model.at[c, 0:12], "hand2")
+    gone(r_core2.at[0:8], "swap3")
+    gone(r_core2.at[0:8], "swap4")
+    when(late, lambda: gone(r_core2, "ag2o"))
+    when(extra, lambda: gone(r_core2, "xgo"))
     for ref, name in ((q_in, "qx"), (x_in, "x")):
         when(extra, lambda ref=ref, name=name: gone(ref.at[0:3], name))
         when(jnp.logical_not(extra), lambda ref=ref, name=name: gone(ref.at[0:4], name))
@@ -506,7 +544,7 @@
             V((256, 256), F32), V((8, 256), F32), V((31, 1, 31), F32), pltpu.SMEM((1, 8), jnp.int32),
             V((32, 128), F32), V((48, 128), F32), op, op, op, op,
             V((384, 256), F32), V((384, 256), F32), V((352, 256), F32), V((352, 256), F32),
-            blocks(18, 2), blocks(18, 2), V((2, 2, 384, 512), BF), V((2, 2, 352, 512), BF), V((2, 2, 2, 144, 512), BF),
+            V((2, 2, 384, 512), BF), V((2, 2, 352, 512), BF),
             blocks(2, 16), blocks(2, 4), blocks(2, 4), blocks(2, 20), V((48, 256), F32), V((48, 256), F32), blocks(44),
             V((8, 256), F32),
             lanes(2, 20), lanes(20), lanes(20), lanes(15), lanes(15),

time: 48.7 us -> 46.5 us (0.955)
  Pallas kernels: 47.2 us -> 45 us
    pallas_call x1, Pallas kernels: 47.2 us -> 45 us  [body(): pl.pallas_call(kernel, out_shape=jax.ShapeDtypeStruct((8, 256), F32), in_...]
where the time goes in v5:
time: 46.5 us; the launch traced here: 46.3 us
  Pallas kernels  45 us (97%)
  local copies, waits for them, and re-layouts  1.3 us (3%)
    pallas_call x1, Pallas kernels, body(): pl.pallas_call(kernel, out_shape=jax.ShapeDtypeStruct((8, 256), F32), in_...  45 us
    unnamed x1, local copies, waits for them, and re-layouts  1.3 us

profile of v5, /device:TPU:6, one launch (start us, length us, event | category | flops | bytes accessed | tf_op | source)
XLA Modules:
  0.0 46.3 jit_solution(16075006197137246681)
XLA Ops:
  0.0 45.0 %shard_map.46 = f32[8,256]{1,0:T(8,128)} custom-call(f32[1,256,256]{2,1,0:T(8,128)} %exp_hbm.1, f32[8,256]{1,0:T(8,128)} %sky_hbm.1, f32[31,1,31]{2,1,0:T(1,128)} %bitcast.1, s32[1,8]{1,0:T(1,128)} %cov_hbm.1), custom_call_target="tpu_custom_call" | custom-call | tf_op jit(solution)/shard_map/pallas_call | solution.py:538
  45.0 1.3 %copy.6 = f32[8,256]{1,0:T(8,128)} copy(f32[8,256]{1,0:T(8,128)} %shard_map.46) | data formatting | bytes 16384

commit v6 on v5

--- a/solution.py
+++ b/solution.py
@@ -124,11 +124,11 @@
 
 
 def is_extra(u):
-    return (u == 5) | (u == 6) | (u == 9) | (u == 10)
+    return (u >= 6) & (u < 10)
 
 
 def extra_pair(u):
-    return jnp.where(u < 8, u - 5, u + 9)
+    return jnp.where(u < 8, u - 6, u + 10)
 
 
 def kernel(
@@ -412,8 +412,8 @@
     @pl.when(extra)
     def _():
         got(x_in, "x")
-        before = prev[c, jnp.where(u < 8, u - 3, 2)]
-        after = follow[c, jnp.where(u < 8, 0, u - 9)]
+        before = prev[c, jnp.where(u < 8, u - 4, 2)]
+        after = follow[c, jnp.where(u < 8, 0, u - 8)]
         exists = jnp.where(u < 8, has_down.astype(jnp.int32), has_up.astype(jnp.int32)) > 0
         old = jnp.where(u < 8, before, after)
         new = old * total_of(a_sum[pair], x_in) / norms[...]

time: 46.5 us -> 46.1 us (level)
  Pallas kernels: 45 us -> 44.5 us
where the time goes in v6:
time: 46.1 us; the launch traced here: 45.8 us
  Pallas kernels  44.5 us (97%)
  local copies, waits for them, and re-layouts  1.3 us (3%)
    pallas_call x1, Pallas kernels, body(): pl.pallas_call(kernel, out_shape=jax.ShapeDtypeStruct((8, 256), F32), in_...  44.5 us
    unnamed x1, local copies, waits for them, and re-layouts  1.3 us

profile of v6, /device:TPU:6, one launch (start us, length us, event | category | flops | bytes accessed | tf_op | source)
XLA Modules:
  0.0 45.8 jit_solution(11321807613656386365)
XLA Ops:
  0.0 44.5 %shard_map.46 = f32[8,256]{1,0:T(8,128)} custom-call(f32[1,256,256]{2,1,0:T(8,128)} %exp_hbm.1, f32[8,256]{1,0:T(8,128)} %sky_hbm.1, f32[31,1,31]{2,1,0:T(1,128)} %bitcast.1, s32[1,8]{1,0:T(1,128)} %cov_hbm.1), custom_call_target="tpu_custom_call" | custom-call | tf_op jit(solution)/shard_map/pallas_call | solution.py:538
  44.5 1.3 %copy.6 = f32[8,256]{1,0:T(8,128)} copy(f32[8,256]{1,0:T(8,128)} %shard_map.46) | data formatting | bytes 16384

commit v7 on v6

--- a/solution.py
+++ b/solution.py
@@ -149,9 +149,6 @@
 
     def there(d):
         return {"visit": 2 * chip(d) + c, "tile": t}
-
-    def across(d):
-        return {"visit": 2 * chip(d) + 1 - c, "tile": t}
 
     partner = {"visit": 2 * u + (1 - c), "tile": t}
     up = {"visit": v, "tile": t + 1}
@@ -404,11 +401,6 @@
     for d in AWAY:
         remote(mine, mine, "ag2", there(d), arrival).start()
 
-    @pl.when(late)
-    def _():
-        for d in AWAY + [(0, 0)]:
-            remote(mine, mine, "ag2o", across(d)).start()
-
     @pl.when(extra)
     def _():
         got(x_in, "x")
@@ -421,8 +413,6 @@
         block = model.at[c, pair]
         for d in AWAY:
             remote(block, block, "xg", there(d)).start()
-        for d in AWAY + [(0, 0)]:
-            remote(block, block, "xgo", across(d)).start()
 
     def got_all(ref, count, mine_too, name):
         when(mine_too, lambda: got(ref.at[c, 0 : count - 1], name))
@@ -447,6 +437,11 @@
     for k in range(2):
         nums2[k, 4:12] = found[:, k]
     remote(nums2.at[1 - c, 4:12], r_core2.at[4:12], "swap3", partner).start()
+    got_all(model, 4, late, "ag2_late")
+    got_all(model, 4, extra, "xg")
+    for name, at in (("ag2o", 0), ("xgo", 16)):
+        part = model.at[c, at : at + 4]
+        remote(part, part, name, partner).start()
     got(r_core2.at[4:12], "swap3")
     a_sum2[4:12] = nums2[c, 4:12] + r_core2[4:12]
     spread = [remote(a_sum2.at[chip(d)], r_in2.at[i], "rs2", there(d)) for i, d in enumerate(AWAY)]
@@ -457,8 +452,6 @@
     for d, copy in zip(AWAY, spread):
         when(inner(chip(d)), copy.start)
 
-    got_all(model, 4, late, "ag2_late")
-    got_all(model, 4, extra, "xg")
     got(model.at[c, 0:4], "ag2o")
     got(model.at[c, 0:4], "xgo")
     put(weave(model, 0, 4), 0, mid, near)
@@ -507,8 +500,8 @@
     gone(model.at[c, 0:12], "hand2")
     gone(r_core2.at[0:8], "swap3")
     gone(r_core2.at[0:8], "swap4")
-    when(late, lambda: gone(r_core2, "ag2o"))
-    when(extra, lambda: gone(r_core2, "xgo"))
+    gone(model.at[c, 0:4], "ag2o")
+    gone(model.at[c, 0:4], "xgo")
     for ref, name in ((q_in, "qx"), (x_in, "x")):
         when(extra, lambda ref=ref, name=name: gone(ref.at[0:3], name))
         when(jnp.logical_not(extra), lambda ref=ref, name=name: gone(ref.at[0:4], name))

time: 46.1 us -> 46.1 us (level)
  no operation moved by 1% of the time
where the time goes in v7:
time: 46.1 us; the launch traced here: 45.6 us
  Pallas kernels  44.3 us (96%)
  local copies, waits for them, and re-layouts  1.3 us (3%)
    pallas_call x1, Pallas kernels, body(): pl.pallas_call(kernel, out_shape=jax.ShapeDtypeStruct((8, 256), F32), in_...  44.3 us
    unnamed x1, local copies, waits for them, and re-layouts  1.3 us

profile of v7, /device:TPU:6, one launch (start us, length us, event | category | flops | bytes accessed | tf_op | source)
XLA Modules:
  0.0 45.6 jit_solution(155707384288414775)
XLA Ops:
  0.0 44.3 %shard_map.46 = f32[8,256]{1,0:T(8,128)} custom-call(f32[1,256,256]{2,1,0:T(8,128)} %exp_hbm.1, f32[8,256]{1,0:T(8,128)} %sky_hbm.1, f32[31,1,31]{2,1,0:T(1,128)} %bitcast.1, s32[1,8]{1,0:T(1,128)} %cov_hbm.1), custom_call_target="tpu_custom_call" | custom-call | tf_op jit(solution)/shard_map/pallas_call | solution.py:531
  44.3 1.3 %copy.6 = f32[8,256]{1,0:T(8,128)} copy(f32[8,256]{1,0:T(8,128)} %shard_map.46) | data formatting | bytes 16384
